TPU v7x, 256 devices: a whole 4x4x8 slice. The times are simulated.
256 devices in a mesh: row: 8 (over y, core), col: 32 (over z, x).
Axes of the slice: x: 4, y: 4, z: 8, core: 2. Of those that a mesh axis runs over, the one named last changes fastest.
Arguments:
- field: float32 [32, 256, 16384], P(None, 'row', 'col'), may hold values from -4 to 4
- right_side: float32 [32, 256, 16384], P(None, 'row', 'col'), may hold values from -6 to 6
- kappa: float32 [256, 16384], P('row', 'col'), may hold values from 0.1 to 3
- fronts: bfloat16 [8, 4096, 16384], P(None, 'row', 'col'), may hold values from -2 to 2
Outputs:
- residual: float32 [32, 256, 16384], P(None, 'row', 'col')
- separator_solution: float32 [256, 16384], P('row', 'col')
All inputs are finite; a program needn't handle non-finite values.
Results may differ from a plain program's by a relative error of at most 0.022.
Values sent between devices are 32-bit elements; how exact they have to be, the bound alone decides.
A program may use at most 64 MiB of HBM per device.

v0:
```python
import jax
import jax.numpy as jnp
from jax import lax
from jax.sharding import PartitionSpec as P


def swapped(value, axis, distance):
    mask = 2**distance
    pairs = [(source, source ^ mask) for source in range(lax.axis_size(axis))]
    return lax.ppermute(value, axis, pairs)


def with_halo(cells, sides, width):
    for axis, dim in sides:
        count = lax.axis_size(axis)
        ends = count - 1
        head = lax.slice_in_dim(cells, 0, width, axis=dim)
        tail = lax.slice_in_dim(cells, cells.shape[dim] - width, cells.shape[dim], axis=dim)
        cells = jnp.concatenate(
            [
                lax.ppermute(tail, axis, [(i, (i + 1) % count) for i in range(ends)]),
                cells,
                lax.ppermute(head, axis, [((i + 1) % count, i) for i in range(ends)]),
            ],
            axis=dim,
        )
    return cells


def times_front(value, front):
    return jnp.dot(value.astype(jnp.bfloat16), front, preferred_element_type=jnp.float32)


def times_front_t(value, front):
    return lax.dot_general(
        value.astype(jnp.bfloat16),
        front,
        (((1,), (1,)), ((), ())),
        preferred_element_type=jnp.float32,
    )


def lift_whole(payload, on_col, bit):
    if on_col:
        return swapped(payload, "col", bit)
    return swapped(payload, "row", bit)


def drop_whole(payload, on_col, bit):
    if on_col:
        return swapped(payload, "col", bit)
    return swapped(payload, "row", bit)


def level_place(level, col_bits):
    if level < col_bits:
        owner = lax.axis_index("col")
        return (True, level, jnp.bitwise_and(jnp.right_shift(owner, level), 1) == 0)
    owner = lax.axis_index("row")
    bit = level - col_bits
    return (False, bit, jnp.bitwise_and(jnp.right_shift(owner, bit), 1) == 0)


def forward(states, fronts, col_bits, levels, lift):
    for level in range(levels):
        on_col, bit, lower = level_place(level, col_bits)
        front = fronts[level]
        firsts = [times_front(state, front) for state in states]
        received = [lift(first, on_col, bit) for first in firsts]
        states = [
            jnp.where(lower, first + got, got - first) for first, got in zip(firsts, received)
        ]
    return states


def backward(states, fronts, col_bits, levels, drop):
    for level in range(levels - 1, -1, -1):
        on_col, bit, lower = level_place(level, col_bits)
        front = fronts[level]
        received = [drop(state, on_col, bit) for state in states]
        states = [
            times_front_t(jnp.where(lower, state - got, state + got), front)
            for state, got in zip(states, received)
        ]
    return states


def body(field, right_side, kappa, fronts):
    padded = with_halo(field, (("row", 1), ("col", 2)), 1)
    near = padded[:, 2:, 1:-1] + padded[:, :-2, 1:-1] + padded[:, 1:-1, 2:] + padded[:, 1:-1, :-2]
    residual = right_side - ((4.0 + kappa) * field - near)
    state = residual[:, -1, :]
    col_bits = lax.axis_size("col").bit_length() - 1
    row_bits = lax.axis_size("row").bit_length() - 1
    levels = col_bits + row_bits
    states = forward([state], fronts, col_bits, levels, lift_whole)
    states = backward(states, fronts, col_bits, levels, drop_whole)
    separator_solution = states[0]
    return (residual, separator_solution)


def solution(mesh):
    placed = (P(None, "row", "col"), P(None, "row", "col"), P("row", "col"), P(None, "row", "col"))
    return jax.shard_map(
        body,
        mesh=mesh,
        in_specs=placed,
        out_specs=(P(None, "row", "col"), P("row", "col")),
        check_vma=False,
    )
```

profile of v0, /device:TPU:8, one launch (start us, length us, event | category | flops | bytes accessed | tf_op | source)
XLA Modules:
  0.0 136.4 jit_solution(18203319145108346075)
XLA Ops:
  0.6 3.0 %copy.14 = f32[32,32,512]{2,0,1:T(8,128)S(1)} copy(f32[32,32,512]{2,1,0:T(8,128)} %param.4) | data formatting | bytes 4194304 | tf_op args[0]
  3.6 1.9 %collective-permute-start.1 = (f32[32,1,512]{2,0,1:T(8,128)S(1)}, f32[32,1,512]{2,0,1:T(8,128)S(1)}, u32[]{:S(2)}, u32[]{:S(2)}) collective-permute-start(f32[32,1,512]{2,0,1:T(8,128)S(1)} %get-tuple-element.9), channel_id=1, source_target_pairs={{0,32},{32,64},{64,96},{96,128},{128,160},{160,192},{192,224},{1,3... | collective-permute-start | bytes 196616 | tf_op jit(solution)/shard_map/ppermute | solution.py:21
  5.5 3.6 %collective-permute-start = (f32[32,1,512]{2,0,1:T(8,128)S(1)}, f32[32,1,512]{2,0,1:T(8,128)S(1)}, u32[]{:S(2)}, u32[]{:S(2)}) collective-permute-start(f32[32,1,512]{2,0,1:T(8,128)S(1)} %get-tuple-element.8), channel_id=1, source_target_pairs={{32,0},{64,32},{96,64},{128,96},{160,128},{192,160},{224,192},{33,... | collective-permute-start | bytes 196616 | tf_op jit(solution)/shard_map/ppermute | solution.py:23
  11.1 1.4 %copy-done.3 = f32[32,34,512]{2,0,1:T(8,128)} copy-done((f32[32,34,512]{2,0,1:T(8,128)}, f32[32,34,512]{2,0,1:T(8,128)S(1)}, u32[]{:S(2)}) %copy-start.3) | copy-done | bytes 2228248
  14.8 4.5 %collective-permute-start.3 = (f32[32,34,1]{1,0,2:T(8,128)S(1)}, f32[32,34,1]{1,0,2:T(8,128)S(1)}, u32[]{:S(2)}, u32[]{:S(2)}) collective-permute-start(f32[32,34,1]{1,0,2:T(8,128)S(1)} %copy.22), channel_id=1, source_target_pairs={{0,1},{1,2},{2,3},{3,4},{4,5},{5,6},{6,7},{7,8},{8,9},{9,10},{10,1... | collective-permute-start | bytes 13064 | tf_op jit(solution)/shard_map/ppermute | solution.py:21
  21.4 5.6 %fusion.2 = f32[32,32,512]{2,0,1:T(8,128)S(1)} fusion(f32[32,34,512]{2,0,1:T(8,128)} %copy-done.3, f32[32,34,1]{2,0,1:T(8,128)S(1)} %copy.23, f32[32,34,1]{2,0,1:T(8,128)S(1)} %copy.21, f32[32,32,512]{2,0,1:T(8,128)S(1)} %copy.14, f32[32,1,512]{2,0,1:T(8,128)S(1)} %collective-permute-done.1, f32[32,1,512]{2,0,1:T(8,128)S(1)} %collective-permute-done, ...), kind=kLoop, calls=%fused_computation.3 | loop fusion | flops 5242880 | bytes 8724992 | tf_op jit(solution)/shard_map/sub | solution.py:91
  27.0 1.3 copy-done
  29.6 2.3 %collective-permute-start.4 = (f32[32,512]{1,0:T(8,128)S(1)}, f32[32,512]{1,0:T(8,128)S(1)}, u32[]{:S(2)}, u32[]{:S(2)}) collective-permute-start(f32[32,512]{1,0:T(8,128)S(1)} %fusion.35), channel_id=1, source_target_pairs={{0,1},{1,0},{2,3},{3,2},{4,5},{5,4},{6,7},{7,6},{8,9},{9,8},{10,11... | collective-permute-start | bytes 196616 | tf_op jit(solution)/shard_map/ppermute | solution.py:10
  31.9 2.6 %collective-permute-done.4 = f32[32,512]{1,0:T(8,128)S(1)} collective-permute-done((f32[32,512]{1,0:T(8,128)S(1)}, f32[32,512]{1,0:T(8,128)S(1)}, u32[]{:S(2)}, u32[]{:S(2)}) %collective-permute-start.4) | collective-permute-done | bytes 65568 | tf_op jit(solution)/shard_map/ppermute | solution.py:10
  35.7 4.3 %collective-permute-start.5 = (f32[32,512]{1,0:T(8,128)S(1)}, f32[32,512]{1,0:T(8,128)S(1)}, u32[]{:S(2)}, u32[]{:S(2)}) collective-permute-start(f32[32,512]{1,0:T(8,128)S(1)} %fusion.31), channel_id=1, source_target_pairs={{0,2},{1,3},{2,0},{3,1},{4,6},{5,7},{6,4},{7,5},{8,10},{9,11},{10,... | collective-permute-start | bytes 196616 | tf_op jit(solution)/shard_map/ppermute | solution.py:10
  40.0 2.3 %collective-permute-done.5 = f32[32,512]{1,0:T(8,128)S(1)} collective-permute-done((f32[32,512]{1,0:T(8,128)S(1)}, f32[32,512]{1,0:T(8,128)S(1)}, u32[]{:S(2)}, u32[]{:S(2)}) %collective-permute-start.5) | collective-permute-done | bytes 65568 | tf_op jit(solution)/shard_map/ppermute | solution.py:10
  43.5 5.2 %collective-permute-start.6 = (f32[32,512]{1,0:T(8,128)S(1)}, f32[32,512]{1,0:T(8,128)S(1)}, u32[]{:S(2)}, u32[]{:S(2)}) collective-permute-start(f32[32,512]{1,0:T(8,128)S(1)} %fusion.27), channel_id=1, source_target_pairs={{0,4},{1,5},{2,6},{3,7},{4,0},{5,1},{6,2},{7,3},{8,12},{9,13},{10,... | collective-permute-start | bytes 196616 | tf_op jit(solution)/shard_map/ppermute | solution.py:10
  48.7 2.2 %collective-permute-done.6 = f32[32,512]{1,0:T(8,128)S(1)} collective-permute-done((f32[32,512]{1,0:T(8,128)S(1)}, f32[32,512]{1,0:T(8,128)S(1)}, u32[]{:S(2)}, u32[]{:S(2)}) %collective-permute-start.6) | collective-permute-done | bytes 65568 | tf_op jit(solution)/shard_map/ppermute | solution.py:10
  52.2 3.4 %collective-permute-start.7 = (f32[32,512]{1,0:T(8,128)S(1)}, f32[32,512]{1,0:T(8,128)S(1)}, u32[]{:S(2)}, u32[]{:S(2)}) collective-permute-start(f32[32,512]{1,0:T(8,128)S(1)} %fusion.23), channel_id=1, source_target_pairs={{0,8},{1,9},{2,10},{3,11},{4,12},{5,13},{6,14},{7,15},{8,0},{9,1},... | collective-permute-start | bytes 196616 | tf_op jit(solution)/shard_map/ppermute | solution.py:10
  55.6 2.2 %collective-permute-done.7 = f32[32,512]{1,0:T(8,128)S(1)} collective-permute-done((f32[32,512]{1,0:T(8,128)S(1)}, f32[32,512]{1,0:T(8,128)S(1)}, u32[]{:S(2)}, u32[]{:S(2)}) %collective-permute-start.7) | collective-permute-done | bytes 65568 | tf_op jit(solution)/shard_map/ppermute | solution.py:10
  59.1 9.5 %collective-permute-start.8 = (f32[32,512]{1,0:T(8,128)S(1)}, f32[32,512]{1,0:T(8,128)S(1)}, u32[]{:S(2)}, u32[]{:S(2)}) collective-permute-start(f32[32,512]{1,0:T(8,128)S(1)} %fusion.19), channel_id=1, source_target_pairs={{0,16},{1,17},{2,18},{3,19},{4,20},{5,21},{6,22},{7,23},{8,24},{9,... | collective-permute-start | bytes 196616 | tf_op jit(solution)/shard_map/ppermute | solution.py:10
  68.5 2.2 %collective-permute-done.8 = f32[32,512]{1,0:T(8,128)S(1)} collective-permute-done((f32[32,512]{1,0:T(8,128)S(1)}, f32[32,512]{1,0:T(8,128)S(1)}, u32[]{:S(2)}, u32[]{:S(2)}) %collective-permute-start.8) | collective-permute-done | bytes 65568 | tf_op jit(solution)/shard_map/ppermute | solution.py:10
  74.5 4.3 %collective-permute-done.10 = f32[32,512]{1,0:T(8,128)S(1)} collective-permute-done((f32[32,512]{1,0:T(8,128)S(1)}, f32[32,512]{1,0:T(8,128)S(1)}, u32[]{:S(2)}, u32[]{:S(2)}) %collective-permute-start.10) | collective-permute-done | bytes 65568 | tf_op jit(solution)/shard_map/ppermute | solution.py:10
  80.0 2.4 %collective-permute-start.11 = (f32[32,512]{1,0:T(8,128)S(1)}, f32[32,512]{1,0:T(8,128)S(1)}, u32[]{:S(2)}, u32[]{:S(2)}) collective-permute-start(f32[32,512]{1,0:T(8,128)S(1)} %fusion.7), channel_id=1, source_target_pairs={{0,128},{32,160},{64,192},{96,224},{128,0},{160,32},{192,64},{224,... | collective-permute-start | bytes 196616 | tf_op jit(solution)/shard_map/ppermute | solution.py:10
  82.4 3.4 %collective-permute-done.11 = f32[32,512]{1,0:T(8,128)S(1)} collective-permute-done((f32[32,512]{1,0:T(8,128)S(1)}, f32[32,512]{1,0:T(8,128)S(1)}, u32[]{:S(2)}, u32[]{:S(2)}) %collective-permute-start.11) | collective-permute-done | bytes 65568 | tf_op jit(solution)/shard_map/ppermute | solution.py:10
  85.8 2.7 %collective-permute-start.12 = (f32[32,512]{1,0:T(8,128)S(1)}, f32[32,512]{1,0:T(8,128)S(1)}, u32[]{:S(2)}, u32[]{:S(2)}) collective-permute-start(f32[32,512]{1,0:T(8,128)S(1)} %subtract_select_fusion), channel_id=1, source_target_pairs={{0,128},{32,160},{64,192},{96,224},{128,0},{160,32},{192,64},{224,... | collective-permute-start | bytes 196616 | tf_op jit(solution)/shard_map/ppermute | solution.py:10
  88.5 3.4 %collective-permute-done.12 = f32[32,512]{1,0:T(8,128)S(1)} collective-permute-done((f32[32,512]{1,0:T(8,128)S(1)}, f32[32,512]{1,0:T(8,128)S(1)}, u32[]{:S(2)}, u32[]{:S(2)}) %collective-permute-start.12) | collective-permute-done | bytes 65568 | tf_op jit(solution)/shard_map/ppermute | solution.py:10
  91.8 1.3 fusion.5
  93.4 4.1 %collective-permute-done.13 = f32[32,512]{1,0:T(8,128)S(1)} collective-permute-done((f32[32,512]{1,0:T(8,128)S(1)}, f32[32,512]{1,0:T(8,128)S(1)}, u32[]{:S(2)}, u32[]{:S(2)}) %collective-permute-start.13) | collective-permute-done | bytes 65568 | tf_op jit(solution)/shard_map/ppermute | solution.py:10
  101.3 6.0 %collective-permute-start.15 = (f32[32,512]{1,0:T(8,128)S(1)}, f32[32,512]{1,0:T(8,128)S(1)}, u32[]{:S(2)}, u32[]{:S(2)}) collective-permute-start(f32[32,512]{1,0:T(8,128)S(1)} %fusion.13), channel_id=1, source_target_pairs={{0,16},{1,17},{2,18},{3,19},{4,20},{5,21},{6,22},{7,23},{8,24},{9,... | collective-permute-start | bytes 196616 | tf_op jit(solution)/shard_map/ppermute | solution.py:10
  107.3 2.4 %collective-permute-done.15 = f32[32,512]{1,0:T(8,128)S(1)} collective-permute-done((f32[32,512]{1,0:T(8,128)S(1)}, f32[32,512]{1,0:T(8,128)S(1)}, u32[]{:S(2)}, u32[]{:S(2)}) %collective-permute-start.15) | collective-permute-done | bytes 65568 | tf_op jit(solution)/shard_map/ppermute | solution.py:10
  111.0 5.2 %collective-permute-done.16 = f32[32,512]{1,0:T(8,128)S(1)} collective-permute-done((f32[32,512]{1,0:T(8,128)S(1)}, f32[32,512]{1,0:T(8,128)S(1)}, u32[]{:S(2)}, u32[]{:S(2)}) %collective-permute-start.16) | collective-permute-done | bytes 65568 | tf_op jit(solution)/shard_map/ppermute | solution.py:10
  117.6 4.3 %collective-permute-done.17 = f32[32,512]{1,0:T(8,128)S(1)} collective-permute-done((f32[32,512]{1,0:T(8,128)S(1)}, f32[32,512]{1,0:T(8,128)S(1)}, u32[]{:S(2)}, u32[]{:S(2)}) %collective-permute-start.17) | collective-permute-done | bytes 65568 | tf_op jit(solution)/shard_map/ppermute | solution.py:10
  123.1 5.8 %collective-permute-done.18 = f32[32,512]{1,0:T(8,128)S(1)} collective-permute-done((f32[32,512]{1,0:T(8,128)S(1)}, f32[32,512]{1,0:T(8,128)S(1)}, u32[]{:S(2)}, u32[]{:S(2)}) %collective-permute-start.18) | collective-permute-done | bytes 65568 | tf_op jit(solution)/shard_map/ppermute | solution.py:10
  130.2 2.5 %copy.25 = f32[32,32,512]{2,1,0:T(8,128)} copy(f32[32,32,512]{2,0,1:T(8,128)S(1)} %copy-done.1) | data formatting | bytes 4194304
  132.8 1.7 %collective-permute-done.19 = f32[32,512]{1,0:T(8,128)S(1)} collective-permute-done((f32[32,512]{1,0:T(8,128)S(1)}, f32[32,512]{1,0:T(8,128)S(1)}, u32[]{:S(2)}, u32[]{:S(2)}) %collective-permute-start.19) | collective-permute-done | bytes 65568 | tf_op jit(solution)/shard_map/ppermute | solution.py:10
  134.5 1.9 %fusion.33 = f32[32,512]{1,0:T(8,128)} fusion(bf16[8,512,512]{2,1,0:T(8,128)(2,1)} %param.7, f32[32,512]{1,0:T(8,128)S(1)} %fusion.29, f32[32,512]{1,0:T(8,128)S(1)} %collective-permute-done.19, pred[]{:T(512)S(6)} %eq.32), kind=kOutput, calls=%fused_computation.37 | convolution fusion | flops 16842752 | bytes 720897 | tf_op jit(solution)/shard_map/dot_general | solution.py:35
  (48 shorter events, 26.6 us)
Async XLA Ops:
  0.6 8.6 %copy-start.2 = (f32[32,32,512]{2,1,0:T(8,128)S(1)}, f32[32,32,512]{2,1,0:T(8,128)}, u32[]{:S(2)}) copy-start(f32[32,32,512]{2,1,0:T(8,128)} %param.4) | copy-start | bytes 6291460
  3.6 5.6 %collective-permute-start.1 = (f32[32,1,512]{2,0,1:T(8,128)S(1)}, f32[32,1,512]{2,0,1:T(8,128)S(1)}, u32[]{:S(2)}, u32[]{:S(2)}) collective-permute-start(f32[32,1,512]{2,0,1:T(8,128)S(1)} %get-tuple-element.9), channel_id=1, source_target_pairs={{0,32},{32,64},{64,96},{96,128},{128,160},{160,192},{192,224},{1,3... | collective-permute-start | bytes 196616 | tf_op jit(solution)/shard_map/ppermute | solution.py:21
  5.5 5.5 %collective-permute-start = (f32[32,1,512]{2,0,1:T(8,128)S(1)}, f32[32,1,512]{2,0,1:T(8,128)S(1)}, u32[]{:S(2)}, u32[]{:S(2)}) collective-permute-start(f32[32,1,512]{2,0,1:T(8,128)S(1)} %get-tuple-element.8), channel_id=1, source_target_pairs={{32,0},{64,32},{96,64},{128,96},{160,128},{192,160},{224,192},{33,... | collective-permute-start | bytes 196616 | tf_op jit(solution)/shard_map/ppermute | solution.py:23
  10.5 8.9 %copy-start.4 = (f32[32,512]{1,0:T(8,128)S(1)}, f32[32,512]{1,0:T(8,128)}, u32[]{:S(2)}) copy-start(f32[32,512]{1,0:T(8,128)} %param.6) | copy-start | bytes 196612
  11.1 1.4 %copy-start.3 = (f32[32,34,512]{2,0,1:T(8,128)}, f32[32,34,512]{2,0,1:T(8,128)S(1)}, u32[]{:S(2)}) copy-start(f32[32,34,512]{2,0,1:T(8,128)S(1)} %constant_dynamic-update-slice_fusion) | copy-start | bytes 6684676
  13.1 6.3 %collective-permute-start.2 = (f32[32,34,1]{1,0,2:T(8,128)S(1)}, f32[32,34,1]{1,0,2:T(8,128)S(1)}, u32[]{:S(2)}, u32[]{:S(2)}) collective-permute-start(f32[32,34,1]{1,0,2:T(8,128)S(1)} %copy.20), channel_id=1, source_target_pairs={{1,0},{2,1},{3,2},{4,3},{5,4},{6,5},{7,6},{8,7},{9,8},{10,9},{11,1... | collective-permute-start | bytes 13064 | tf_op jit(solution)/shard_map/ppermute | solution.py:23
  14.8 6.0 %collective-permute-start.3 = (f32[32,34,1]{1,0,2:T(8,128)S(1)}, f32[32,34,1]{1,0,2:T(8,128)S(1)}, u32[]{:S(2)}, u32[]{:S(2)}) collective-permute-start(f32[32,34,1]{1,0,2:T(8,128)S(1)} %copy.22), channel_id=1, source_target_pairs={{0,1},{1,2},{2,3},{3,4},{4,5},{5,6},{6,7},{7,8},{8,9},{9,10},{10,1... | collective-permute-start | bytes 13064 | tf_op jit(solution)/shard_map/ppermute | solution.py:21
  27.0 1.3 copy-start
  29.6 4.9 %collective-permute-start.4 = (f32[32,512]{1,0:T(8,128)S(1)}, f32[32,512]{1,0:T(8,128)S(1)}, u32[]{:S(2)}, u32[]{:S(2)}) collective-permute-start(f32[32,512]{1,0:T(8,128)S(1)} %fusion.35), channel_id=1, source_target_pairs={{0,1},{1,0},{2,3},{3,2},{4,5},{5,4},{6,7},{7,6},{8,9},{9,8},{10,11... | collective-permute-start | bytes 196616 | tf_op jit(solution)/shard_map/ppermute | solution.py:10
  35.7 6.6 %collective-permute-start.5 = (f32[32,512]{1,0:T(8,128)S(1)}, f32[32,512]{1,0:T(8,128)S(1)}, u32[]{:S(2)}, u32[]{:S(2)}) collective-permute-start(f32[32,512]{1,0:T(8,128)S(1)} %fusion.31), channel_id=1, source_target_pairs={{0,2},{1,3},{2,0},{3,1},{4,6},{5,7},{6,4},{7,5},{8,10},{9,11},{10,... | collective-permute-start | bytes 196616 | tf_op jit(solution)/shard_map/ppermute | solution.py:10
  43.5 7.5 %collective-permute-start.6 = (f32[32,512]{1,0:T(8,128)S(1)}, f32[32,512]{1,0:T(8,128)S(1)}, u32[]{:S(2)}, u32[]{:S(2)}) collective-permute-start(f32[32,512]{1,0:T(8,128)S(1)} %fusion.27), channel_id=1, source_target_pairs={{0,4},{1,5},{2,6},{3,7},{4,0},{5,1},{6,2},{7,3},{8,12},{9,13},{10,... | collective-permute-start | bytes 196616 | tf_op jit(solution)/shard_map/ppermute | solution.py:10
  52.2 5.6 %collective-permute-start.7 = (f32[32,512]{1,0:T(8,128)S(1)}, f32[32,512]{1,0:T(8,128)S(1)}, u32[]{:S(2)}, u32[]{:S(2)}) collective-permute-start(f32[32,512]{1,0:T(8,128)S(1)} %fusion.23), channel_id=1, source_target_pairs={{0,8},{1,9},{2,10},{3,11},{4,12},{5,13},{6,14},{7,15},{8,0},{9,1},... | collective-permute-start | bytes 196616 | tf_op jit(solution)/shard_map/ppermute | solution.py:10
  59.1 11.7 %collective-permute-start.8 = (f32[32,512]{1,0:T(8,128)S(1)}, f32[32,512]{1,0:T(8,128)S(1)}, u32[]{:S(2)}, u32[]{:S(2)}) collective-permute-start(f32[32,512]{1,0:T(8,128)S(1)} %fusion.19), channel_id=1, source_target_pairs={{0,16},{1,17},{2,18},{3,19},{4,20},{5,21},{6,22},{7,23},{8,24},{9,... | collective-permute-start | bytes 196616 | tf_op jit(solution)/shard_map/ppermute | solution.py:10
  72.0 1.3 collective-permute-start.9
  74.5 4.3 %collective-permute-start.10 = (f32[32,512]{1,0:T(8,128)S(1)}, f32[32,512]{1,0:T(8,128)S(1)}, u32[]{:S(2)}, u32[]{:S(2)}) collective-permute-start(f32[32,512]{1,0:T(8,128)S(1)} %fusion.11), channel_id=1, source_target_pairs={{0,64},{32,96},{64,0},{96,32},{128,192},{160,224},{192,128},{224,1... | collective-permute-start | bytes 196616 | tf_op jit(solution)/shard_map/ppermute | solution.py:10
  80.0 5.8 %collective-permute-start.11 = (f32[32,512]{1,0:T(8,128)S(1)}, f32[32,512]{1,0:T(8,128)S(1)}, u32[]{:S(2)}, u32[]{:S(2)}) collective-permute-start(f32[32,512]{1,0:T(8,128)S(1)} %fusion.7), channel_id=1, source_target_pairs={{0,128},{32,160},{64,192},{96,224},{128,0},{160,32},{192,64},{224,... | collective-permute-start | bytes 196616 | tf_op jit(solution)/shard_map/ppermute | solution.py:10
  85.8 6.0 %collective-permute-start.12 = (f32[32,512]{1,0:T(8,128)S(1)}, f32[32,512]{1,0:T(8,128)S(1)}, u32[]{:S(2)}, u32[]{:S(2)}) collective-permute-start(f32[32,512]{1,0:T(8,128)S(1)} %subtract_select_fusion), channel_id=1, source_target_pairs={{0,128},{32,160},{64,192},{96,224},{128,0},{160,32},{192,64},{224,... | collective-permute-start | bytes 196616 | tf_op jit(solution)/shard_map/ppermute | solution.py:10
  93.1 37.1 %copy-start.1 = (f32[32,32,512]{2,0,1:T(8,128)S(1)}, f32[32,32,512]{2,0,1:T(8,128)}, u32[]{:S(2)}) copy-start(f32[32,32,512]{2,0,1:T(8,128)} %copy-done) | copy-start | bytes 6291460
  93.1 4.3 %collective-permute-start.13 = (f32[32,512]{1,0:T(8,128)S(1)}, f32[32,512]{1,0:T(8,128)S(1)}, u32[]{:S(2)}, u32[]{:S(2)}) collective-permute-start(f32[32,512]{1,0:T(8,128)S(1)} %fusion.5), channel_id=1, source_target_pairs={{0,64},{32,96},{64,0},{96,32},{128,192},{160,224},{192,128},{224,1... | collective-permute-start | bytes 196616 | tf_op jit(solution)/shard_map/ppermute | solution.py:10
  98.8 1.3 collective-permute-start.14
  101.3 8.4 %collective-permute-start.15 = (f32[32,512]{1,0:T(8,128)S(1)}, f32[32,512]{1,0:T(8,128)S(1)}, u32[]{:S(2)}, u32[]{:S(2)}) collective-permute-start(f32[32,512]{1,0:T(8,128)S(1)} %fusion.13), channel_id=1, source_target_pairs={{0,16},{1,17},{2,18},{3,19},{4,20},{5,21},{6,22},{7,23},{8,24},{9,... | collective-permute-start | bytes 196616 | tf_op jit(solution)/shard_map/ppermute | solution.py:10
  111.0 5.3 %collective-permute-start.16 = (f32[32,512]{1,0:T(8,128)S(1)}, f32[32,512]{1,0:T(8,128)S(1)}, u32[]{:S(2)}, u32[]{:S(2)}) collective-permute-start(f32[32,512]{1,0:T(8,128)S(1)} %fusion.17), channel_id=1, source_target_pairs={{0,8},{1,9},{2,10},{3,11},{4,12},{5,13},{6,14},{7,15},{8,0},{9,1},... | collective-permute-start | bytes 196616 | tf_op jit(solution)/shard_map/ppermute | solution.py:10
  117.5 4.3 %collective-permute-start.17 = (f32[32,512]{1,0:T(8,128)S(1)}, f32[32,512]{1,0:T(8,128)S(1)}, u32[]{:S(2)}, u32[]{:S(2)}) collective-permute-start(f32[32,512]{1,0:T(8,128)S(1)} %fusion.21), channel_id=1, source_target_pairs={{0,4},{1,5},{2,6},{3,7},{4,0},{5,1},{6,2},{7,3},{8,12},{9,13},{10,... | collective-permute-start | bytes 196616 | tf_op jit(solution)/shard_map/ppermute | solution.py:10
  123.1 5.8 %collective-permute-start.18 = (f32[32,512]{1,0:T(8,128)S(1)}, f32[32,512]{1,0:T(8,128)S(1)}, u32[]{:S(2)}, u32[]{:S(2)}) collective-permute-start(f32[32,512]{1,0:T(8,128)S(1)} %fusion.25), channel_id=1, source_target_pairs={{0,2},{1,3},{2,0},{3,1},{4,6},{5,7},{6,4},{7,5},{8,10},{9,11},{10,... | collective-permute-start | bytes 196616 | tf_op jit(solution)/shard_map/ppermute | solution.py:10
  130.2 4.3 %collective-permute-start.19 = (f32[32,512]{1,0:T(8,128)S(1)}, f32[32,512]{1,0:T(8,128)S(1)}, u32[]{:S(2)}, u32[]{:S(2)}) collective-permute-start(f32[32,512]{1,0:T(8,128)S(1)} %fusion.29), channel_id=1, source_target_pairs={{0,1},{1,0},{2,3},{3,2},{4,5},{5,4},{6,7},{7,6},{8,9},{9,8},{10,11... | collective-permute-start | bytes 196616 | tf_op jit(solution)/shard_map/ppermute | solution.py:10
where the time goes:
time: 137 us; the launch traced here: 136 us
  waiting for transfers between devices  50 us (36%)
  starting transfers between devices  47.5 us (35%)
  matrix products  20.8 us (15%)
  local copies, waits for them, and re-layouts  11.7 us (9%)
  other arithmetic  5.64 us (4%)
    ppermute x16, waiting for transfers between devices, swapped(): return lax.ppermute(value, axis, pairs)  48.6 us
    ppermute x16, starting transfers between devices, swapped(): return lax.ppermute(value, axis, pairs)  36.1 us
    dot_general x8, matrix products, times_front_t(): lax.dot_general(value.astype(jnp.bfloat16), front, (((1,), (1,)), ((), ()...  11 us
    dot_general x8, matrix products, times_front(): jnp.dot(value.astype(jnp.bfloat16), front, preferred_element_type=jnp.flo...  9.81 us
    unnamed x14, local copies, waits for them, and re-layouts  9.44 us
    ppermute x2, starting transfers between devices, with_halo(): lax.ppermute(tail, axis, [(i, (i + 1) % count) for i in range(ends)])  6.46 us
    sub x1, other arithmetic, body(): residual = right_side - ((4.0 + kappa) * field - near)  5.62 us
    ppermute x2, starting transfers between devices, with_halo(): lax.ppermute(head, axis, [((i + 1) % count, i) for i in range(ends)])  4.93 us
  transfers between devices with their start and end apart: 20, of which 18 were waited for; matrix products, arithmetic and copies ran while one was open for 4% of the time, Pallas kernels for 0%

commit v1 on v0

v1 whole, which is shorter than its diff:
```python
import functools

import jax
import jax.numpy as jnp
from jax import lax
from jax.experimental import pallas as pl
from jax.experimental.pallas import tpu as pltpu
from jax.sharding import PartitionSpec as P

MESH = pl.DeviceIdType.MESH
LANES = 128
CHUNKS = 4


def kernel(
    sizes,
    field, right_side, kappa, fronts,
    residual, separator,
    cells, sources, shift, result, weights,
    first_row, last_row, below, above, edge_left, edge_right,
    rim_first, rim_last, rim_left, rim_right,
    sent, got,
    load_sem, front_sem, store_sem, halo_send, halo_recv, send_sem, recv_sem,
):
    k_count, depth, width, levels, col_bits, n_row, n_col = sizes
    row = lax.axis_index("row")
    col = lax.axis_index("col")
    rows_per = k_count // CHUNKS

    def partner(level):
        if level < col_bits:
            return {"col": jnp.bitwise_xor(col, 1 << level)}
        return {"row": jnp.bitwise_xor(row, 1 << (level - col_bits))}

    def sign(level):
        place = col if level < col_bits else row
        bit = level if level < col_bits else level - col_bits
        upper = jnp.bitwise_and(jnp.right_shift(place, bit), 1)
        return 1.0 - 2.0 * upper.astype(jnp.float32)

    up = {"row": lax.rem(row + n_row - 1, n_row)}
    down = {"row": lax.rem(row + 1, n_row)}
    left = {"col": lax.rem(col + n_col - 1, n_col)}
    right = {"col": lax.rem(col + 1, n_col)}

    barrier = pltpu.get_barrier_semaphore()
    friends = [partner(level) for level in range(levels)] + [up, down, left, right]
    for friend in friends:
        pl.semaphore_signal(barrier, inc=1, device_id=friend, device_id_type=MESH)

    loads = [
        pltpu.make_async_copy(field, cells, load_sem.at[0]),
        pltpu.make_async_copy(right_side, sources, load_sem.at[1]),
        pltpu.make_async_copy(kappa, shift, load_sem.at[2]),
    ]
    for load in loads:
        load.start()
    front_loads = [
        pltpu.make_async_copy(fronts.at[level], weights.at[level], front_sem.at[level])
        for level in range(levels)
    ]
    for load in front_loads:
        load.start()

    def halo(slot, source, target, device):
        return pltpu.make_async_remote_copy(
            src_ref=source,
            dst_ref=target,
            send_sem=halo_send.at[slot],
            recv_sem=halo_recv.at[slot],
            device_id=device,
            device_id_type=MESH,
        )

    halos = [
        halo(0, first_row, below, up),
        halo(1, last_row.at[:, pl.ds(width - LANES, LANES)], edge_left, right),
        halo(2, last_row.at[:, pl.ds(0, LANES)], edge_right, left),
        halo(3, last_row, above, down),
        halo(4, rim_last, rim_left, right),
        halo(5, rim_first, rim_right, left),
    ]

    loads[0].wait()
    first_row[...] = cells[:, 0, :]
    last_row[...] = cells[:, depth - 1, :]
    pl.semaphore_wait(barrier, len(friends))
    for slot in range(4):
        halos[slot].start()

    rim_lane = lax.broadcasted_iota(jnp.int32, (depth, LANES), 1)
    firsts = jnp.zeros((depth, LANES), jnp.float32)
    lasts = jnp.zeros((depth, LANES), jnp.float32)
    for k in range(k_count):
        head = cells[k, :, pl.ds(0, LANES)]
        tail = cells[k, :, pl.ds(width - LANES, LANES)]
        firsts = jnp.where(rim_lane == k, pltpu.roll(head, k, 1) if k else head, firsts)
        lasts = jnp.where(rim_lane == k, pltpu.roll(tail, k + 1, 1), lasts)
    rim_first[...] = firsts
    rim_last[...] = lasts
    halos[4].start()
    halos[5].start()

    has_above = (row > 0).astype(jnp.float32)
    has_below = (row < n_row - 1).astype(jnp.float32)
    has_left = (col > 0).astype(jnp.float32)
    has_right = (col < n_col - 1).astype(jnp.float32)

    def beside(block, right_edge, left_edge):
        lane = lax.broadcasted_iota(jnp.int32, block.shape, 1)
        from_right = jnp.where(lane == width - 1, right_edge, pltpu.roll(block, width - 1, 1))
        from_left = jnp.where(lane == 0, left_edge, pltpu.roll(block, 1, 1))
        return from_right, from_left

    def level_step(stage, chunk, state, level, transposed):
        dims = (((1,), (1,)), ((), ())) if transposed else (((1,), (0,)), ((), ()))
        return lax.dot_general(
            state.astype(jnp.bfloat16),
            weights[level],
            dims,
            preferred_element_type=jnp.float32,
        )

    exchanges = 2 * levels - 1

    def exchange(index, chunk):
        level = index if index < levels else 2 * levels - 2 - index
        part = pl.ds(chunk * rows_per, rows_per)
        return pltpu.make_async_remote_copy(
            src_ref=sent.at[index, part],
            dst_ref=got.at[index, part],
            send_sem=send_sem.at[index, chunk],
            recv_sem=recv_sem.at[index, chunk],
            device_id=partner(level),
            device_id_type=MESH,
        )

    def piece(k):
        block = cells[k]
        line = lax.broadcasted_iota(jnp.int32, block.shape, 0)
        under = jnp.where(
            line == depth - 1, below[pl.ds(k, 1), :] * has_below, pltpu.roll(block, depth - 1, 0)
        )
        over = jnp.where(line == 0, above[pl.ds(k, 1), :] * has_above, pltpu.roll(block, 1, 0))
        from_right, from_left = beside(
            block,
            rim_right[:, pl.ds(k, 1)] * has_right,
            rim_left[:, pl.ds(k, 1)] * has_left,
        )
        near = under + over + from_right + from_left
        result[k] = sources[k] - ((4.0 + shift[...]) * block - near)

    for load in loads[1:]:
        load.wait()
    shift_last = shift[pl.ds(depth - 1, 1), :]
    for slot in range(3):
        halos[slot].wait_recv()

    for chunk in range(CHUNKS):
        part = pl.ds(chunk * rows_per, rows_per)
        block = last_row[part, :]
        over = cells[part, depth - 2, :]
        source = sources[part, depth - 1, :]
        under = below[part, :] * has_below
        from_right, from_left = beside(
            block,
            edge_right[part, pl.ds(0, 1)] * has_right,
            edge_left[part, pl.ds(LANES - 1, 1)] * has_left,
        )
        near = under + over + from_right + from_left
        state = source - ((4.0 + shift_last) * block - near)
        if chunk == 0:
            front_loads[0].wait()
        sent[0, part] = level_step(0, chunk, state, 0, False)
        exchange(0, chunk).start()

    for slot in range(3, 6):
        halos[slot].wait_recv()

    pieces = list(range(k_count))
    slots = max(1, (exchanges - 1) * CHUNKS)
    done = 0
    gap = 0
    for stage in range(1, exchanges + 1):
        index = stage - 1
        forward = stage < levels
        level = stage if forward else 2 * levels - 1 - stage
        if forward:
            front_loads[level].wait()
        for chunk in range(CHUNKS):
            part = pl.ds(chunk * rows_per, rows_per)
            exchange(index, chunk).wait_recv()
            other = got[index, part]
            if forward:
                state = other + sign(level - 1) * sent[index, part]
            elif stage == levels:
                state = 2.0 * other
            else:
                state = sent[index, part] - sign(level) * other
            product = level_step(stage, chunk, state, level, not forward)
            if stage < exchanges:
                sent[stage, part] = product
                exchange(stage, chunk).start()
                gap += 1
                while pieces and done * slots < gap * k_count:
                    piece(pieces.pop(0))
                    done += 1
                    if done == k_count:
                        store = pltpu.make_async_copy(result, residual, store_sem)
                        store.start()
            else:
                separator[part, :] = product

    store.wait()
    for slot in range(6):
        halos[slot].wait_send()
    for index in range(exchanges):
        for chunk in range(CHUNKS):
            exchange(index, chunk).wait_send()


def body(field, right_side, kappa, fronts):
    k_count, depth, width = field.shape
    n_row = lax.axis_size("row")
    n_col = lax.axis_size("col")
    col_bits = n_col.bit_length() - 1
    levels = col_bits + n_row.bit_length() - 1
    exchanges = 2 * levels - 1
    f32 = jnp.float32
    whole = pl.BlockSpec(memory_space=pl.ANY)
    dma = pltpu.SemaphoreType.DMA
    residual, separator = pl.pallas_call(
        functools.partial(kernel, (k_count, depth, width, levels, col_bits, n_row, n_col)),
        out_shape=(
            jax.ShapeDtypeStruct((k_count, depth, width), f32),
            jax.ShapeDtypeStruct((k_count, width), f32),
        ),
        in_specs=[pl.BlockSpec(memory_space=pltpu.HBM)] * 4,
        out_specs=(whole, pl.BlockSpec(memory_space=pltpu.VMEM)),
        scratch_shapes=[
            pltpu.VMEM((k_count, depth, width), f32),
            pltpu.VMEM((k_count, depth, width), f32),
            pltpu.VMEM((depth, width), f32),
            pltpu.VMEM((k_count, depth, width), f32),
            pltpu.VMEM((levels, width, width), jnp.bfloat16),
            pltpu.VMEM((k_count, width), f32),
            pltpu.VMEM((k_count, width), f32),
            pltpu.VMEM((k_count, width), f32),
            pltpu.VMEM((k_count, width), f32),
            pltpu.VMEM((k_count, LANES), f32),
            pltpu.VMEM((k_count, LANES), f32),
            pltpu.VMEM((depth, LANES), f32),
            pltpu.VMEM((depth, LANES), f32),
            pltpu.VMEM((depth, LANES), f32),
            pltpu.VMEM((depth, LANES), f32),
            pltpu.VMEM((exchanges, k_count, width), f32),
            pltpu.VMEM((exchanges, k_count, width), f32),
            dma((3,)),
            dma((levels,)),
            dma,
            dma((6,)),
            dma((6,)),
            dma((exchanges, CHUNKS)),
            dma((exchanges, CHUNKS)),
        ],
        compiler_params=pltpu.CompilerParams(
            collective_id=0, has_side_effects=True, vmem_limit_bytes=67043328
        ),
    )(
        field,
        right_side,
        kappa,
        fronts,
    )
    return (residual, separator)


def solution(mesh):
    placed = (P(None, "row", "col"), P(None, "row", "col"), P("row", "col"), P(None, "row", "col"))
    return jax.shard_map(
        body,
        mesh=mesh,
        in_specs=placed,
        out_specs=(P(None, "row", "col"), P("row", "col")),
        check_vma=False,
    )
```

time: 137 us -> 72.7 us (0.53)
  Pallas kernels: 0 us -> 68.1 us
  waiting for transfers between devices: 50 us -> 0 us
  starting transfers between devices: 47.5 us -> 0 us
  matrix products: 20.8 us -> 0 us
  local copies, waits for them, and re-layouts: 11.7 us -> 3.85 us
  other arithmetic: 5.64 us -> 0 us
    pallas_call x0 -> x1, Pallas kernels: none -> 68.1 us  [body(): pl.pallas_call(functools.partial(kernel, (k_count, depth, width, levels,...]
    ppermute x20 -> x0, waiting for transfers between devices: 50 us -> none  [the longest x16 48.6 us: swapped(): return lax.ppermute(value, axis, pairs)]
    ppermute x20 -> x0, starting transfers between devices: 47.5 us -> none  [the longest x16 36.1 us: swapped(): return lax.ppermute(value, axis, pairs)]
    dot_general x16 -> x0, matrix products: 20.8 us -> none  [the longest x8 11 us: times_front_t(): lax.dot_general(value.astype(jnp.bfloat16), front, (((1,), (1,)), ((), ()...]
    sub x1 -> x0, other arithmetic: 5.62 us -> none  [body(): residual = right_side - ((4.0 + kappa) * field - near)]
    unnamed x14 -> x4, local copies, waits for them, and re-layouts: 9.44 us -> 3.85 us
  transfers between devices with their start and end apart: 20 -> 0, of which waited for: 18 -> 0; matrix products, arithmetic and copies ran while one was open for 4% -> 0% of each run, Pallas kernels for 0% -> 0%
where the time goes in v1:
time: 72.7 us; the launch traced here: 72.6 us
  Pallas kernels  68.1 us (94%)
  local copies, waits for them, and re-layouts  3.85 us (5%)
    pallas_call x1, Pallas kernels, body(): pl.pallas_call(functools.partial(kernel, (k_count, depth, width, levels,...  68.1 us
    unnamed x4, local copies, waits for them, and re-layouts  3.85 us

profile of v1, /device:TPU:8, one launch (start us, length us, event | category | flops | bytes accessed | tf_op | source)
XLA Modules:
  0.0 72.6 jit_solution(12665603552324228056)
XLA Ops:
  0.6 68.1 %shard_map.59 = (f32[32,32,512]{2,1,0:T(8,128)}, f32[32,512]{1,0:T(8,128)}) custom-call(f32[32,32,512]{2,1,0:T(8,128)} %field.1, f32[32,32,512]{2,1,0:T(8,128)} %right_side.1, f32[32,512]{1,0:T(8,128)} %kappa.1, bf16[8,512,512]{2,1,0:T(8,128)(2,1)} %fronts.1), custom_call_target="tpu_custom_call" | custom-call | tf_op jit(solution)/shard_map/pallas_call | solution.py:232
  68.7 0.0 copy-start
  68.7 3.2 %copy.8 = f32[32,32,512]{2,1,0:T(8,128)} copy(f32[32,32,512]{2,1,0:T(8,128)} %get-tuple-element.4) | data formatting | bytes 4194304
  71.9 0.0 copy-done
  71.9 0.6 copy.9
Async XLA Ops:
  68.7 3.2 %copy-start = (f32[32,512]{1,0:T(8,128)S(1)}, f32[32,512]{1,0:T(8,128)}, u32[]{:S(2)}) copy-start(f32[32,512]{1,0:T(8,128)} %get-tuple-element.5) | copy-start | bytes 196612

commit v2 on v1

v2 whole, which is shorter than its diff:
```python
import functools

import jax
import jax.numpy as jnp
from jax import lax
from jax.experimental import pallas as pl
from jax.experimental.pallas import tpu as pltpu
from jax.sharding import PartitionSpec as P

MESH = pl.DeviceIdType.MESH
LANES = 128
CHUNKS = 4
PIECE = 32


def back_groups(levels, col_bits):
    groups = []
    level = levels - 1
    while level >= 0:
        row_pair = level == levels - 1 and level - 1 >= col_bits
        col_pair = level % 2 == 1 and level < col_bits and level <= 3
        if row_pair or col_pair:
            groups.append((level, level - 1))
            level -= 2
        else:
            groups.append((level,))
            level -= 1
    return groups


def group_targets(group, top):
    if len(group) == 1:
        return [group]
    a, b = group
    return [(a,), (a, b)] if top else [(a,), (b,), (a, b)]


def phase_plan(levels, col_bits):
    groups = back_groups(levels, col_bits)
    targets = [[(level,)] for level in range(levels - 1)]
    targets.append(group_targets(groups[0], True))
    for group in groups[1:]:
        targets.append(group_targets(group, False))
    return groups, targets


def kernel(
    sizes,
    field, right_side, kappa, fronts,
    residual, separator,
    cells, sources, shift, weights, extra, bulk_out, bulk_in,
    first_row, last_row, below, above, edge_left, edge_right,
    rim_first, rim_last, rim_left, rim_right,
    sent, got,
    load_sem, front_sem, halo_send, halo_recv, send_sem, recv_sem, bulk_send, bulk_recv,
    col_ready, row_ready,
):
    k_count, depth, width, levels, col_bits, n_row, n_col = sizes
    row = lax.axis_index("row")
    col = lax.axis_index("col")
    rows_per = k_count // CHUNKS
    groups, targets = phase_plan(levels, col_bits)
    phases = len(targets)
    pairs = [group for group in groups if len(group) == 2]
    row_bits = levels - col_bits
    piece_count = width // PIECE

    def flip(toggled):
        if toggled[0] < col_bits:
            return {"col": jnp.bitwise_xor(col, sum(1 << level for level in toggled))}
        return {"row": jnp.bitwise_xor(row, sum(1 << (level - col_bits) for level in toggled))}

    def sign(level):
        place = col if level < col_bits else row
        bit = level if level < col_bits else level - col_bits
        upper = jnp.bitwise_and(jnp.right_shift(place, bit), 1)
        return 1.0 - 2.0 * upper.astype(jnp.float32)

    def row_at(step):
        return {"row": lax.rem(row + (n_row + step) % n_row, n_row)}

    def col_at(step):
        return {"col": lax.rem(col + (n_col + step) % n_col, n_col)}

    up, down, left, right = row_at(-1), row_at(1), col_at(-1), col_at(1)

    barrier = pltpu.get_barrier_semaphore()
    friends = [up, down, left, right] + [flip((b,)) for a, b in pairs]
    for friend in friends:
        pl.semaphore_signal(barrier, inc=1, device_id=friend, device_id_type=MESH)

    def tell(step):
        for ready, at, bits in ((col_ready, col_at, col_bits), (row_ready, row_at, row_bits)):
            if step < bits:
                for way, sense in ((0, 1), (1, -1)):
                    pl.semaphore_signal(
                        ready.at[step, way],
                        inc=1,
                        device_id=at(sense * (1 << (step - 1))),
                        device_id_type=MESH,
                    )

    def hear(step):
        for ready, bits in ((col_ready, col_bits), (row_ready, row_bits)):
            if step < bits:
                for way in range(2):
                    pl.semaphore_wait(ready.at[step, way], 1)

    loads = [
        pltpu.make_async_copy(field, cells, load_sem.at[0]),
        pltpu.make_async_copy(right_side, sources, load_sem.at[1]),
        pltpu.make_async_copy(kappa, shift, load_sem.at[2]),
    ]
    front_loads = [
        pltpu.make_async_copy(fronts.at[level], weights.at[level], front_sem.at[level])
        for level in range(levels)
    ]
    loads[0].start()
    front_loads[0].start()
    loads[1].start()
    loads[2].start()
    order = [pair[0] for pair in pairs]
    order += [level for level in range(1, levels) if level not in order]
    for level in order:
        front_loads[level].start()

    def halo(slot, source, target, device):
        return pltpu.make_async_remote_copy(
            src_ref=source,
            dst_ref=target,
            send_sem=halo_send.at[slot],
            recv_sem=halo_recv.at[slot],
            device_id=device,
            device_id_type=MESH,
        )

    def chunk_rows(chunk):
        return pl.ds(chunk * rows_per, rows_per)

    edge_halos = [
        halo(0, last_row.at[:, pl.ds(width - LANES, LANES)], edge_left, right),
        halo(1, last_row.at[:, pl.ds(0, LANES)], edge_right, left),
    ]
    rim_halos = [
        halo(2, rim_last, rim_left, right),
        halo(3, rim_first, rim_right, left),
    ]
    above_halo = halo(4, last_row, above, down)
    below_halos = [
        halo(5 + chunk, first_row.at[chunk_rows(chunk)], below.at[chunk_rows(chunk)], up)
        for chunk in range(CHUNKS)
    ]

    def bulk(pair, piece):
        part = pl.ds(piece * PIECE, PIECE)
        return pltpu.make_async_remote_copy(
            src_ref=bulk_out.at[pair, part],
            dst_ref=bulk_in.at[pair, part],
            send_sem=bulk_send.at[pair, piece],
            recv_sem=bulk_recv.at[pair, piece],
            device_id=flip((pairs[pair][1],)),
            device_id_type=MESH,
        )

    def bulk_start(pair, piece):
        part = pl.ds(piece * PIECE, PIECE)
        bulk_out[pair, part] = weights[pairs[pair][0], part].astype(jnp.float32)
        bulk(pair, piece).start()

    def bulk_take(pair, piece):
        part = pl.ds(piece * PIECE, PIECE)
        bulk(pair, piece).wait_recv()
        extra[pair, part] = bulk_in[pair, part].astype(jnp.bfloat16)

    loads[0].wait()
    first_row[...] = cells[:, 0, :]
    last_row[...] = cells[:, depth - 1, :]
    pl.semaphore_wait(barrier, len(friends))
    for copy in edge_halos + below_halos:
        copy.start()
    tell(1)
    above_halo.start()

    rim_lane = lax.broadcasted_iota(jnp.int32, (depth, LANES), 1)
    firsts = jnp.zeros((depth, LANES), jnp.float32)
    lasts = jnp.zeros((depth, LANES), jnp.float32)
    for k in range(k_count):
        head = cells[k, :, pl.ds(0, LANES)]
        tail = cells[k, :, pl.ds(width - LANES, LANES)]
        firsts = jnp.where(rim_lane == k, pltpu.roll(head, k, 1) if k else head, firsts)
        lasts = jnp.where(rim_lane == k, pltpu.roll(tail, k + 1, 1), lasts)
    rim_first[...] = firsts
    rim_last[...] = lasts
    for copy in rim_halos:
        copy.start()

    has_above = (row > 0).astype(jnp.float32)
    has_below = (row < n_row - 1).astype(jnp.float32)
    has_left = (col > 0).astype(jnp.float32)
    has_right = (col < n_col - 1).astype(jnp.float32)

    def beside(block, right_edge, left_edge):
        lane = lax.broadcasted_iota(jnp.int32, block.shape, 1)
        from_right = jnp.where(lane == width - 1, right_edge, pltpu.roll(block, width - 1, 1))
        from_left = jnp.where(lane == 0, left_edge, pltpu.roll(block, 1, 1))
        return from_right, from_left

    def times(state, front):
        return lax.dot_general(
            state.astype(jnp.bfloat16),
            front,
            (((1,), (0,)), ((), ())),
            preferred_element_type=jnp.float32,
        )

    def times_t(state, front):
        return lax.dot_general(
            state.astype(jnp.bfloat16),
            front,
            (((1,), (1,)), ((), ())),
            preferred_element_type=jnp.float32,
        )

    def exchange(phase, slot, chunk):
        part = chunk_rows(chunk)
        return pltpu.make_async_remote_copy(
            src_ref=sent.at[phase, part],
            dst_ref=got.at[phase, slot, part],
            send_sem=send_sem.at[phase, slot, chunk],
            recv_sem=recv_sem.at[phase, slot, chunk],
            device_id=flip(targets[phase][slot]),
            device_id_type=MESH,
        )

    def send(phase, chunk, value):
        sent[phase, chunk_rows(chunk)] = value
        for slot in range(len(targets[phase])):
            exchange(phase, slot, chunk).start()

    def receive(phase, chunk):
        values = []
        for slot in range(len(targets[phase])):
            exchange(phase, slot, chunk).wait_recv()
            values.append(got[phase, slot, chunk_rows(chunk)])
        return values

    def piece(k):
        block = cells[k]
        line = lax.broadcasted_iota(jnp.int32, block.shape, 0)
        under = jnp.where(
            line == depth - 1, below[pl.ds(k, 1), :] * has_below, pltpu.roll(block, depth - 1, 0)
        )
        over = jnp.where(line == 0, above[pl.ds(k, 1), :] * has_above, pltpu.roll(block, 1, 0))
        from_right, from_left = beside(
            block,
            rim_right[:, pl.ds(k, 1)] * has_right,
            rim_left[:, pl.ds(k, 1)] * has_left,
        )
        near = under + over + from_right + from_left
        residual[k] = sources[k] - ((4.0 + shift[...]) * block - near)

    work = [[] for _ in range(phases)]

    def plan(first, last, tasks):
        spots = list(range(max(0, first), min(last, phases - 1) + 1))
        for index, task in enumerate(tasks):
            work[spots[index * len(spots) // len(tasks)]].append(task)

    early = []
    for number, (a, b) in enumerate(pairs):
        starts = [functools.partial(bulk_start, number, p) for p in range(piece_count)]
        takes = [functools.partial(bulk_take, number, p) for p in range(piece_count)]
        use = [at for at in range(levels - 1, phases) if groups[at - levels + 1] == (a, b)][0]
        if number == 0 and a >= col_bits:
            early += starts[:5]
            plan(0, levels - 3, starts[5:])
            plan(levels - 2, levels - 1, takes)
        elif a >= 2:
            early += starts[:4]
            plan(0, 1, starts[4:8])
            plan(col_bits, use - 2, starts[8:])
            plan(use, use, takes)
        else:
            plan(2, use - 1, starts)
            plan(use, use, takes)
    plan(2, phases - 1, [functools.partial(piece, k) for k in range(k_count)])

    def fill(phase, chunk):
        tasks = work[phase]
        for index, task in enumerate(tasks):
            if index * CHUNKS // len(tasks) == chunk:
                task()

    for a, b in pairs:
        front_loads[a].wait()
    for task in early:
        task()

    loads[1].wait()
    loads[2].wait()
    front_loads[0].wait()
    shift_last = shift[pl.ds(depth - 1, 1), :]
    for copy in edge_halos:
        copy.wait_recv()
    for chunk in range(CHUNKS):
        part = chunk_rows(chunk)
        block = last_row[part, :]
        from_right, from_left = beside(
            block,
            edge_right[part, pl.ds(0, 1)] * has_right,
            edge_left[part, pl.ds(LANES - 1, 1)] * has_left,
        )
        below_halos[chunk].wait_recv()
        near = below[part, :] * has_below + cells[part, depth - 2, :] + from_right + from_left
        state = sources[part, depth - 1, :] - ((4.0 + shift_last) * block - near)
        send(0, chunk, times(state, weights[0]))
        fill(0, chunk)

    waited = [0] + [a for a, b in pairs]
    for level in range(1, levels):
        if level not in waited:
            front_loads[level].wait()
        hear(level)
        tell(level + 1)
        if level == 1:
            above_halo.wait_recv()
            for copy in rim_halos:
                copy.wait_recv()
        for chunk in range(CHUNKS):
            (other,) = receive(level - 1, chunk)
            state = other + sign(level - 1) * sent[level - 1, chunk_rows(chunk)]
            send(level, chunk, times(state, weights[level]))
            fill(level, chunk)

    for number, group in enumerate(groups):
        phase = levels - 1 + number
        if len(group) == 2:
            a, b = group
            spare = pairs.index(group)
        for chunk in range(CHUNKS):
            part = chunk_rows(chunk)
            values = receive(phase, chunk)
            mine = sent[phase, part]
            if len(group) == 1:
                mix = 2.0 * values[0] if number == 0 else mine - sign(group[0]) * values[0]
                product = times_t(mix, weights[group[0]])
            else:
                if number == 0:
                    here = 2.0 * values[0]
                    there = 2.0 * values[1]
                else:
                    here = mine - sign(a) * values[0]
                    there = values[1] - sign(a) * values[2]
                here = times_t(here, weights[a])
                there = times_t(there, extra[spare])
                product = times_t(here - sign(b) * there, weights[b])
            if phase + 1 < phases:
                send(phase + 1, chunk, product)
                fill(phase + 1, chunk)
            else:
                separator[part, :] = product

    for copy in edge_halos + rim_halos + [above_halo] + below_halos:
        copy.wait_send()
    for pair in range(len(pairs)):
        for number in range(piece_count):
            bulk(pair, number).wait_send()
    for phase in range(phases):
        for slot in range(len(targets[phase])):
            for chunk in range(CHUNKS):
                exchange(phase, slot, chunk).wait_send()


def body(field, right_side, kappa, fronts):
    k_count, depth, width = field.shape
    n_row = lax.axis_size("row")
    n_col = lax.axis_size("col")
    col_bits = n_col.bit_length() - 1
    levels = col_bits + n_row.bit_length() - 1
    groups, targets = phase_plan(levels, col_bits)
    phases = len(targets)
    slots = max(len(target) for target in targets)
    pairs = sum(len(group) == 2 for group in groups)
    f32 = jnp.float32
    dma = pltpu.SemaphoreType.DMA
    regular = pltpu.SemaphoreType.REGULAR
    cube = pltpu.VMEM((k_count, depth, width), f32)
    line = pltpu.VMEM((k_count, width), f32)
    edge = pltpu.VMEM((k_count, LANES), f32)
    rim = pltpu.VMEM((depth, LANES), f32)
    arrays = (field, right_side, kappa, fronts)
    return pl.pallas_call(
        functools.partial(kernel, (k_count, depth, width, levels, col_bits, n_row, n_col)),
        out_shape=(
            jax.ShapeDtypeStruct((k_count, depth, width), f32),
            jax.ShapeDtypeStruct((k_count, width), f32),
        ),
        in_specs=[pl.BlockSpec(memory_space=pl.ANY)] * 4,
        out_specs=(pl.BlockSpec(memory_space=pltpu.VMEM),) * 2,
        scratch_shapes=[
            cube,
            cube,
            pltpu.VMEM((depth, width), f32),
            pltpu.VMEM((levels, width, width), jnp.bfloat16),
            pltpu.VMEM((pairs, width, width), jnp.bfloat16),
            pltpu.VMEM((pairs, width, width), f32),
            pltpu.VMEM((pairs, width, width), f32),
            line, line, line, line,
            edge, edge,
            rim, rim, rim, rim,
            pltpu.VMEM((phases, k_count, width), f32),
            pltpu.VMEM((phases, slots, k_count, width), f32),
            dma((3,)),
            dma((levels,)),
            dma((5 + CHUNKS,)),
            dma((5 + CHUNKS,)),
            dma((phases, slots, CHUNKS)),
            dma((phases, slots, CHUNKS)),
            dma((pairs, width // PIECE)),
            dma((pairs, width // PIECE)),
            regular((col_bits, 2)),
            regular((levels - col_bits, 2)),
        ],
        compiler_params=pltpu.CompilerParams(
            collective_id=0, has_side_effects=True, vmem_limit_bytes=40 << 20
        ),
    )(*(pltpu.with_memory_space_constraint(array, pltpu.HBM) for array in arrays))


def solution(mesh):
    placed = (P(None, "row", "col"), P(None, "row", "col"), P("row", "col"), P(None, "row", "col"))
    return jax.shard_map(
        body,
        mesh=mesh,
        in_specs=placed,
        out_specs=(P(None, "row", "col"), P("row", "col")),
        check_vma=False,
    )
```

time: 72.7 us -> 65.9 us (0.906)
  Pallas kernels: 68.1 us -> 63 us
  local copies, waits for them, and re-layouts: 3.85 us -> 1.95 us
    pallas_call x1, Pallas kernels: 68.1 us -> 63 us  [body(): pl.pallas_call(functools.partial(kernel, (k_count, depth, width, levels,...]
    unnamed x4 -> x2, local copies, waits for them, and re-layouts: 3.85 us -> 1.95 us
where the time goes in v2:
time: 65.9 us; the launch traced here: 65.6 us
  Pallas kernels  63 us (96%)
  local copies, waits for them, and re-layouts  1.95 us (3%)
    pallas_call x1, Pallas kernels, body(): pl.pallas_call(functools.partial(kernel, (k_count, depth, width, levels,...  63 us
    unnamed x2, local copies, waits for them, and re-layouts  1.95 us

profile of v2, /device:TPU:8, one launch (start us, length us, event | category | flops | bytes accessed | tf_op | source)
XLA Modules:
  0.0 65.6 jit_solution(11783280833043148497)
XLA Ops:
  0.6 63.0 %shard_map.59 = (f32[32,32,512]{2,1,0:T(8,128)S(1)}, f32[32,512]{1,0:T(8,128)S(1)}) custom-call(f32[32,32,512]{2,1,0:T(8,128)} %field.1, f32[32,32,512]{2,1,0:T(8,128)} %right_side.1, f32[32,512]{1,0:T(8,128)} %kappa.1, bf16[8,512,512]{2,1,0:T(8,128)(2,1)} %fronts.1), custom_call_target="tpu_custom_call" | custom-call | tf_op jit(solution)/shard_map/pallas_call | solution.py:392
  63.7 1.3 %copy.8 = f32[32,32,512]{2,1,0:T(8,128)} copy(f32[32,32,512]{2,1,0:T(8,128)S(1)} %get-tuple-element.4) | data formatting | bytes 4194304
  65.0 0.6 copy.9

commit v3 on v2

--- a/solution.py
+++ b/solution.py
@@ -37,8 +37,7 @@
 
 def phase_plan(levels, col_bits):
     groups = back_groups(levels, col_bits)
-    targets = [[(level,)] for level in range(levels - 1)]
-    targets.append(group_targets(groups[0], True))
+    targets = [group_targets(groups[0], True)]
     for group in groups[1:]:
         targets.append(group_targets(group, False))
     return groups, targets
@@ -48,12 +47,12 @@
     sizes,
     field, right_side, kappa, fronts,
     residual, separator,
-    cells, sources, shift, weights, extra, bulk_out, bulk_in,
+    cells, sources, shift, weights, turned, extra, bulk_out, bulk_in,
     first_row, last_row, below, above, edge_left, edge_right,
     rim_first, rim_last, rim_left, rim_right,
-    sent, got,
+    sent, got, level_zero, first_got, pair_sent, pair_got, top_sent, hop_out, hop_in, twin,
     load_sem, front_sem, halo_send, halo_recv, send_sem, recv_sem, bulk_send, bulk_recv,
-    col_ready, row_ready,
+    col_ready, row_ready, first_send, first_recv, pair_send, pair_recv, hop_send, hop_recv,
 ):
     k_count, depth, width, levels, col_bits, n_row, n_col = sizes
     row = lax.axis_index("row")
@@ -85,7 +84,10 @@
     up, down, left, right = row_at(-1), row_at(1), col_at(-1), col_at(1)
 
     barrier = pltpu.get_barrier_semaphore()
-    friends = [up, down, left, right] + [flip((b,)) for a, b in pairs]
+    core = lax.rem(row, 2)
+    other_core = {"row": jnp.bitwise_xor(row, 1)}
+    across = {"row": jnp.bitwise_xor(row, 1), "col": jnp.bitwise_xor(col, 1)}
+    friends = [up, down, left, right, across] + [flip((b,)) for a, b in pairs]
     for friend in friends:
         pl.semaphore_signal(barrier, inc=1, device_id=friend, device_id_type=MESH)
 
@@ -119,7 +121,7 @@
     front_loads[0].start()
     loads[1].start()
     loads[2].start()
-    order = [pair[0] for pair in pairs]
+    order = [1] + [a for a, b in pairs if a != 1]
     order += [level for level in range(1, levels) if level not in order]
     for level in order:
         front_loads[level].start()
@@ -164,13 +166,17 @@
 
     def bulk_start(pair, piece):
         part = pl.ds(piece * PIECE, PIECE)
-        bulk_out[pair, part] = weights[pairs[pair][0], part].astype(jnp.float32)
+        bulk_out[pair, part] = turned[pairs[pair][0], part].astype(jnp.float32)
         bulk(pair, piece).start()
 
     def bulk_take(pair, piece):
         part = pl.ds(piece * PIECE, PIECE)
         bulk(pair, piece).wait_recv()
         extra[pair, part] = bulk_in[pair, part].astype(jnp.bfloat16)
+
+    def turn(level, block):
+        part = pl.ds(block * LANES, LANES)
+        turned[level, part, :] = weights[level, :, part].T
 
     loads[0].wait()
     first_row[...] = cells[:, 0, :]
@@ -213,14 +219,6 @@
             preferred_element_type=jnp.float32,
         )
 
-    def times_t(state, front):
-        return lax.dot_general(
-            state.astype(jnp.bfloat16),
-            front,
-            (((1,), (1,)), ((), ())),
-            preferred_element_type=jnp.float32,
-        )
-
     def exchange(phase, slot, chunk):
         part = chunk_rows(chunk)
         return pltpu.make_async_remote_copy(
@@ -259,40 +257,108 @@
         near = under + over + from_right + from_left
         residual[k] = sources[k] - ((4.0 + shift[...]) * block - near)
 
-    work = [[] for _ in range(phases)]
-
-    def plan(first, last, tasks):
-        spots = list(range(max(0, first), min(last, phases - 1) + 1))
+    top_level = levels - 1
+    local = col_bits
+
+    def first(slot, chunk):
+        part = chunk_rows(chunk)
+        return pltpu.make_async_remote_copy(
+            src_ref=level_zero.at[part],
+            dst_ref=first_got.at[slot, part],
+            send_sem=first_send.at[slot, chunk],
+            recv_sem=first_recv.at[slot, chunk],
+            device_id=(other_core, across, flip((0,)))[slot],
+            device_id_type=MESH,
+        )
+
+    def pair_copy(level, chunk):
+        return pltpu.make_async_remote_copy(
+            src_ref=pair_sent.at[level, chunk],
+            dst_ref=pair_got.at[level, chunk],
+            send_sem=pair_send.at[level, chunk],
+            recv_sem=pair_recv.at[level, chunk],
+            device_id=flip((level,)),
+            device_id_type=MESH,
+        )
+
+    def top_copy(owner, slot, chunk):
+        part = chunk_rows(chunk)
+        steps = sum(1 << (level - col_bits) for level in targets[0][slot])
+        return pltpu.make_async_remote_copy(
+            src_ref=top_sent.at[owner, part],
+            dst_ref=got.at[0, slot, part],
+            send_sem=send_sem.at[0, slot, owner * CHUNKS + chunk],
+            recv_sem=recv_sem.at[0, slot, chunk],
+            device_id={"row": jnp.bitwise_xor(row, steps + 1 - owner)},
+            device_id_type=MESH,
+        )
+
+    hop_pieces = width // LANES
+
+    def hop(level, piece):
+        part = pl.ds(piece * LANES, LANES)
+        return pltpu.make_async_remote_copy(
+            src_ref=hop_out.at[level % 2, part],
+            dst_ref=hop_in.at[level, part],
+            send_sem=hop_send.at[level, piece],
+            recv_sem=hop_recv.at[level, piece],
+            device_id=other_core,
+            device_id_type=MESH,
+        )
+
+    def hop_start(level):
+        for number in range(hop_pieces):
+            part = pl.ds(number * LANES, LANES)
+            hop_out[level % 2, part] = weights[level, part].astype(jnp.float32)
+            hop(level, number).start()
+
+    def hop_sent(level):
+        for number in range(hop_pieces):
+            hop(level, number).wait_send()
+
+    def hop_take(level):
+        for number in range(hop_pieces):
+            part = pl.ds(number * LANES, LANES)
+            hop(level, number).wait_recv()
+            twin[level, part] = hop_in[level, part].astype(jnp.bfloat16)
+
+    def spread(tasks, spots):
+        out = [[] for _ in range(spots)]
         for index, task in enumerate(tasks):
-            work[spots[index * len(spots) // len(tasks)]].append(task)
-
+            out[index * spots // len(tasks)].append(task)
+        return out
+
+    starts = []
+    takes = []
+    for number in range(len(pairs)):
+        starts.append([functools.partial(bulk_start, number, p) for p in range(piece_count)])
+        takes.append([functools.partial(bulk_take, number, p) for p in range(piece_count)])
+    blocks = width // LANES
+    ready_turns = [a for a, b in pairs if a != 1]
     early = []
     for number, (a, b) in enumerate(pairs):
-        starts = [functools.partial(bulk_start, number, p) for p in range(piece_count)]
-        takes = [functools.partial(bulk_take, number, p) for p in range(piece_count)]
-        use = [at for at in range(levels - 1, phases) if groups[at - levels + 1] == (a, b)][0]
-        if number == 0 and a >= col_bits:
-            early += starts[:5]
-            plan(0, levels - 3, starts[5:])
-            plan(levels - 2, levels - 1, takes)
-        elif a >= 2:
-            early += starts[:4]
-            plan(0, 1, starts[4:8])
-            plan(col_bits, use - 2, starts[8:])
-            plan(use, use, takes)
-        else:
-            plan(2, use - 1, starts)
-            plan(use, use, takes)
-    plan(2, phases - 1, [functools.partial(piece, k) for k in range(k_count)])
-
-    def fill(phase, chunk):
-        tasks = work[phase]
-        for index, task in enumerate(tasks):
-            if index * CHUNKS // len(tasks) == chunk:
-                task()
+        if a != 1:
+            quick = 5 if a >= col_bits else 4
+            early += starts[number][:quick]
+            starts[number] = starts[number][quick:]
+    late_turns = [
+        [functools.partial(turn, level, block) for block in range(blocks)]
+        for level in range(levels)
+        if level not in ready_turns and level != 1
+    ]
+    residual_tasks = [functools.partial(piece, k) for k in range(k_count)]
+
+    front_loads[1].wait()
+
+    @pl.when(core == 0)
+    def _():
+        hop_start(1)
 
     for a, b in pairs:
-        front_loads[a].wait()
+        if a != 1:
+            front_loads[a].wait()
+            for block in range(blocks):
+                turn(a, block)
     for task in early:
         task()
 
@@ -313,37 +379,172 @@
         below_halos[chunk].wait_recv()
         near = below[part, :] * has_below + cells[part, depth - 2, :] + from_right + from_left
         state = sources[part, depth - 1, :] - ((4.0 + shift_last) * block - near)
-        send(0, chunk, times(state, weights[0]))
-        fill(0, chunk)
-
-    waited = [0] + [a for a, b in pairs]
-    for level in range(1, levels):
-        if level not in waited:
+        product = times(state, weights[0])
+        level_zero[part, :] = product
+
+        @pl.when(core == 0)
+        def _():
+            first(1, chunk).start()
+            first(0, chunk).start()
+
+        @pl.when(core == 1)
+        def _():
+            first(2, chunk).start()
+
+    for level in range(2, levels):
+        if level not in ready_turns:
             front_loads[level].wait()
-        hear(level)
-        tell(level + 1)
-        if level == 1:
-            above_halo.wait_recv()
-            for copy in rim_halos:
-                copy.wait_recv()
+    above_halo.wait_recv()
+    for copy in rim_halos:
+        copy.wait_recv()
+
+    @pl.when(core == 0)
+    def _():
+        for level in range(1, levels):
+            hear(level)
+            tell(level + 1)
+        steps = list(range(2, levels))
+        plans = [[] for _ in steps]
+        rest = []
+        for number, (a, b) in enumerate(pairs):
+            if a >= col_bits:
+                for at, tasks in enumerate(spread(starts[number], len(steps))):
+                    plans[at] += tasks
+            elif a != 1:
+                rest += starts[number]
+            else:
+                rest = [functools.partial(turn, 1, block) for block in range(blocks)] + rest + starts[number]
+        for at, tasks in enumerate(spread(sum(late_turns, []) + residual_tasks, len(steps))):
+            plans[at] += tasks
+        for at, level in enumerate(steps):
+            if level >= 3:
+                hop_sent(level - 2)
+            hop_start(level)
+            for task in plans[at]:
+                task()
+        for task in rest:
+            task()
+        if pairs[0][0] >= col_bits:
+            for task in takes[0]:
+                task()
+        for level in range(max(1, levels - 2), levels):
+            hop_sent(level)
+        for slot in range(2):
+            for chunk in range(CHUNKS):
+                first(slot, chunk).wait_send()
+
+    @pl.when(core == 1)
+    def _():
+        stages = [level for level in range(1, levels) if level != local + 1]
+        plans = [[] for _ in stages]
+
+        def add(first_level, last_level, tasks):
+            spots = [at for at, level in enumerate(stages) if first_level <= level <= last_level]
+            spots = spots or [len(stages) - 1]
+            for at, part in zip(spots, spread(tasks, len(spots))):
+                plans[at] += part
+
+        for number, (a, b) in enumerate(pairs):
+            if a >= col_bits:
+                add(1, levels - 2, starts[number])
+                add(levels - 1, levels - 1, takes[number])
+            elif a != 1:
+                add(1, 1, starts[number][:4])
+                add(local, levels - 1, starts[number][4:])
+            else:
+                add(1, 1, [functools.partial(turn, 1, block) for block in range(blocks)])
+                add(2, levels - 1, starts[number])
+        for at, tasks in enumerate(late_turns):
+            add(2 + at, 2 + at, tasks)
+        add(2, levels - 1, residual_tasks[:k_count // 2])
+
+        def fill(tasks, chunk):
+            for index, task in enumerate(tasks):
+                if index * CHUNKS // len(tasks) == chunk:
+                    task()
+
+        hop_take(1)
+        for at, level in enumerate(stages):
+            hear(level)
+            tell(level + 1)
+            if level == local:
+                hear(level + 1)
+                tell(level + 2)
+            for chunk in range(CHUNKS):
+                part = chunk_rows(chunk)
+                sense = sign(level - 1)
+                if level == 1:
+                    for slot in range(3):
+                        first(slot, chunk).wait_recv()
+                    low = first_got[1, part] + sense * first_got[0, part]
+                    high = first_got[2, part] + sense * level_zero[part, :]
+                else:
+                    past = level - 1
+                    pair_copy(past, chunk).wait_recv()
+                    both = pair_got[past, chunk] + sense * pair_sent[past, chunk]
+                    low = both[:rows_per]
+                    high = both[rows_per:]
+                low = times(low, twin[level])
+                high = times(high, weights[level])
+                out = level
+                if level == local:
+                    low, high = low + high, low - high
+                    out = level + 1
+                    low = times(low, twin[out])
+                    high = times(high, weights[out])
+                if out == top_level:
+                    for owner, value in enumerate((low, high)):
+                        top_sent[owner, part] = value
+                        for slot in range(len(targets[0])):
+                            top_copy(owner, slot, chunk).start()
+                else:
+                    pair_sent[out, chunk, pl.ds(0, rows_per)] = low
+                    pair_sent[out, chunk, pl.ds(rows_per, rows_per)] = high
+                    pair_copy(out, chunk).start()
+                fill(plans[at], chunk)
+            if out < top_level:
+                hop_take(out + 1)
+                if out + 1 == local:
+                    hop_take(out + 2)
         for chunk in range(CHUNKS):
-            (other,) = receive(level - 1, chunk)
-            state = other + sign(level - 1) * sent[level - 1, chunk_rows(chunk)]
-            send(level, chunk, times(state, weights[level]))
-            fill(level, chunk)
+            first(2, chunk).wait_send()
+            for level in range(1, top_level):
+                if level != local:
+                    pair_copy(level, chunk).wait_send()
+            for owner in range(2):
+                for slot in range(len(targets[0])):
+                    top_copy(owner, slot, chunk).wait_send()
+
+    work = [[] for _ in range(phases)]
+    for number, (a, b) in enumerate(pairs):
+        if a < col_bits:
+            work[groups.index((a, b))] += takes[number]
+
+    def fill_back(phase, chunk):
+        tasks = work[phase]
+        for index, task in enumerate(tasks):
+            if index * CHUNKS // len(tasks) == chunk:
+                task()
+
+        @pl.when(core == 1)
+        def _():
+            later = residual_tasks[k_count // 2:]
+            for index, task in enumerate(later):
+                if index * (phases - 1) * CHUNKS // len(later) == (phase - 1) * CHUNKS + chunk:
+                    task()
 
     for number, group in enumerate(groups):
-        phase = levels - 1 + number
+        phase = number
         if len(group) == 2:
             a, b = group
             spare = pairs.index(group)
         for chunk in range(CHUNKS):
             part = chunk_rows(chunk)
             values = receive(phase, chunk)
-            mine = sent[phase, part]
+            mine = sent[phase, part] if number else None
             if len(group) == 1:
                 mix = 2.0 * values[0] if number == 0 else mine - sign(group[0]) * values[0]
-                product = times_t(mix, weights[group[0]])
+                product = times(mix, turned[group[0]])
             else:
                 if number == 0:
                     here = 2.0 * values[0]
@@ -351,12 +552,12 @@
                 else:
                     here = mine - sign(a) * values[0]
                     there = values[1] - sign(a) * values[2]
-                here = times_t(here, weights[a])
-                there = times_t(there, extra[spare])
-                product = times_t(here - sign(b) * there, weights[b])
+                here = times(here, turned[a])
+                there = times(there, extra[spare])
+                product = times(here - sign(b) * there, turned[b])
             if phase + 1 < phases:
                 send(phase + 1, chunk, product)
-                fill(phase + 1, chunk)
+                fill_back(phase + 1, chunk)
             else:
                 separator[part, :] = product
 
@@ -365,7 +566,7 @@
     for pair in range(len(pairs)):
         for number in range(piece_count):
             bulk(pair, number).wait_send()
-    for phase in range(phases):
+    for phase in range(1, phases):
         for slot in range(len(targets[phase])):
             for chunk in range(CHUNKS):
                 exchange(phase, slot, chunk).wait_send()
@@ -402,6 +603,7 @@
             cube,
             pltpu.VMEM((depth, width), f32),
             pltpu.VMEM((levels, width, width), jnp.bfloat16),
+            pltpu.VMEM((levels, width, width), jnp.bfloat16),
             pltpu.VMEM((pairs, width, width), jnp.bfloat16),
             pltpu.VMEM((pairs, width, width), f32),
             pltpu.VMEM((pairs, width, width), f32),
@@ -410,19 +612,33 @@
             rim, rim, rim, rim,
             pltpu.VMEM((phases, k_count, width), f32),
             pltpu.VMEM((phases, slots, k_count, width), f32),
+            line,
+            pltpu.VMEM((3, k_count, width), f32),
+            pltpu.VMEM((levels, CHUNKS, 2 * k_count // CHUNKS, width), f32),
+            pltpu.VMEM((levels, CHUNKS, 2 * k_count // CHUNKS, width), f32),
+            pltpu.VMEM((2, k_count, width), f32),
+            pltpu.VMEM((2, width, width), f32),
+            pltpu.VMEM((levels, width, width), f32),
+            pltpu.VMEM((levels, width, width), jnp.bfloat16),
             dma((3,)),
             dma((levels,)),
             dma((5 + CHUNKS,)),
             dma((5 + CHUNKS,)),
-            dma((phases, slots, CHUNKS)),
+            dma((phases, slots, 2 * CHUNKS)),
             dma((phases, slots, CHUNKS)),
             dma((pairs, width // PIECE)),
             dma((pairs, width // PIECE)),
             regular((col_bits, 2)),
             regular((levels - col_bits, 2)),
+            dma((3, CHUNKS)),
+            dma((3, CHUNKS)),
+            dma((levels, CHUNKS)),
+            dma((levels, CHUNKS)),
+            dma((levels, width // LANES)),
+            dma((levels, width // LANES)),
         ],
         compiler_params=pltpu.CompilerParams(
-            collective_id=0, has_side_effects=True, vmem_limit_bytes=40 << 20
+            collective_id=0, has_side_effects=True, vmem_limit_bytes=48 << 20
         ),
     )(*(pltpu.with_memory_space_constraint(array, pltpu.HBM) for array in arrays))
 

time: 65.9 us -> 68.9 us (1.046)
  Pallas kernels: 63 us -> 65.8 us
    pallas_call x1, Pallas kernels: 63 us -> 65.8 us  [body(): pl.pallas_call(functools.partial(kernel, (k_count, depth, width, levels,...]
where the time goes in v3:
time: 68.9 us; the launch traced here: 68.4 us
  Pallas kernels  65.8 us (96%)
  local copies, waits for them, and re-layouts  1.95 us (3%)
    pallas_call x1, Pallas kernels, body(): pl.pallas_call(functools.partial(kernel, (k_count, depth, width, levels,...  65.8 us
    unnamed x2, local copies, waits for them, and re-layouts  1.95 us

profile of v3, /device:TPU:8, one launch (start us, length us, event | category | flops | bytes accessed | tf_op | source)
XLA Modules:
  0.0 68.4 jit_solution(1937399346959007072)
XLA Ops:
  0.6 65.8 %shard_map.59 = (f32[32,32,512]{2,1,0:T(8,128)S(1)}, f32[32,512]{1,0:T(8,128)S(1)}) custom-call(f32[32,32,512]{2,1,0:T(8,128)} %field.1, f32[32,32,512]{2,1,0:T(8,128)} %right_side.1, f32[32,512]{1,0:T(8,128)} %kappa.1, bf16[8,512,512]{2,1,0:T(8,128)(2,1)} %fronts.1), custom_call_target="tpu_custom_call" | custom-call | tf_op jit(solution)/shard_map/pallas_call | solution.py:593
  66.4 1.3 %copy.8 = f32[32,32,512]{2,1,0:T(8,128)} copy(f32[32,32,512]{2,1,0:T(8,128)S(1)} %get-tuple-element.4) | data formatting | bytes 4194304
  67.8 0.6 copy.9

commit v4 on v3

--- a/solution.py
+++ b/solution.py
@@ -9,7 +9,10 @@
 
 MESH = pl.DeviceIdType.MESH
 LANES = 128
-CHUNKS = 4
+CHUNKS = 2
+HOP_SLOTS = 4
+X_STEP = 1
+Y_EARLY = 16
 PIECE = 32
 
 
@@ -18,7 +21,7 @@
     level = levels - 1
     while level >= 0:
         row_pair = level == levels - 1 and level - 1 >= col_bits
-        col_pair = level % 2 == 1 and level < col_bits and level <= 3
+        col_pair = level % 2 == 1 and level < col_bits and level <= 1
         if row_pair or col_pair:
             groups.append((level, level - 1))
             level -= 2
@@ -121,7 +124,7 @@
     front_loads[0].start()
     loads[1].start()
     loads[2].start()
-    order = [1] + [a for a, b in pairs if a != 1]
+    order = [1, 2] + [a for a, b in pairs if a != 1]
     order += [level for level in range(1, levels) if level not in order]
     for level in order:
         front_loads[level].start()
@@ -298,7 +301,7 @@
     def hop(level, piece):
         part = pl.ds(piece * LANES, LANES)
         return pltpu.make_async_remote_copy(
-            src_ref=hop_out.at[level % 2, part],
+            src_ref=hop_out.at[level % HOP_SLOTS, part],
             dst_ref=hop_in.at[level, part],
             send_sem=hop_send.at[level, piece],
             recv_sem=hop_recv.at[level, piece],
@@ -309,7 +312,7 @@
     def hop_start(level):
         for number in range(hop_pieces):
             part = pl.ds(number * LANES, LANES)
-            hop_out[level % 2, part] = weights[level, part].astype(jnp.float32)
+            hop_out[level % HOP_SLOTS, part] = weights[level, part].astype(jnp.float32)
             hop(level, number).start()
 
     def hop_sent(level):
@@ -338,9 +341,8 @@
     early = []
     for number, (a, b) in enumerate(pairs):
         if a != 1:
-            quick = 5 if a >= col_bits else 4
-            early += starts[number][:quick]
-            starts[number] = starts[number][quick:]
+            early += starts[number][:Y_EARLY]
+            starts[number] = starts[number][Y_EARLY:]
     late_turns = [
         [functools.partial(turn, level, block) for block in range(blocks)]
         for level in range(levels)
@@ -353,6 +355,8 @@
     @pl.when(core == 0)
     def _():
         hop_start(1)
+        front_loads[2].wait()
+        hop_start(2)
 
     for a, b in pairs:
         if a != 1:
@@ -391,7 +395,11 @@
         def _():
             first(2, chunk).start()
 
-    for level in range(2, levels):
+    @pl.when(core == 1)
+    def _():
+        front_loads[2].wait()
+
+    for level in range(3, levels):
         if level not in ready_turns:
             front_loads[level].wait()
     above_halo.wait_recv()
@@ -403,22 +411,26 @@
         for level in range(1, levels):
             hear(level)
             tell(level + 1)
-        steps = list(range(2, levels))
+        steps = list(range(3, levels))
         plans = [[] for _ in steps]
         rest = []
+
+        def add(first_step, tasks):
+            spots = len(steps) - min(first_step, len(steps) - 1)
+            for at, part in enumerate(spread(tasks, spots)):
+                plans[len(steps) - spots + at] += part
+
         for number, (a, b) in enumerate(pairs):
             if a >= col_bits:
-                for at, tasks in enumerate(spread(starts[number], len(steps))):
-                    plans[at] += tasks
-            elif a != 1:
-                rest += starts[number]
+                add(0, starts[number])
             else:
-                rest = [functools.partial(turn, 1, block) for block in range(blocks)] + rest + starts[number]
+                add(0, [functools.partial(turn, 1, block) for block in range(blocks)])
+                add(X_STEP, starts[number])
         for at, tasks in enumerate(spread(sum(late_turns, []) + residual_tasks, len(steps))):
             plans[at] += tasks
         for at, level in enumerate(steps):
-            if level >= 3:
-                hop_sent(level - 2)
+            if level > HOP_SLOTS:
+                hop_sent(level - HOP_SLOTS)
             hop_start(level)
             for task in plans[at]:
                 task()
@@ -427,7 +439,7 @@
         if pairs[0][0] >= col_bits:
             for task in takes[0]:
                 task()
-        for level in range(max(1, levels - 2), levels):
+        for level in range(max(1, levels - HOP_SLOTS), levels):
             hop_sent(level)
         for slot in range(2):
             for chunk in range(CHUNKS):
@@ -448,9 +460,6 @@
             if a >= col_bits:
                 add(1, levels - 2, starts[number])
                 add(levels - 1, levels - 1, takes[number])
-            elif a != 1:
-                add(1, 1, starts[number][:4])
-                add(local, levels - 1, starts[number][4:])
             else:
                 add(1, 1, [functools.partial(turn, 1, block) for block in range(blocks)])
                 add(2, levels - 1, starts[number])
@@ -617,7 +626,7 @@
             pltpu.VMEM((levels, CHUNKS, 2 * k_count // CHUNKS, width), f32),
             pltpu.VMEM((levels, CHUNKS, 2 * k_count // CHUNKS, width), f32),
             pltpu.VMEM((2, k_count, width), f32),
-            pltpu.VMEM((2, width, width), f32),
+            pltpu.VMEM((HOP_SLOTS, width, width), f32),
             pltpu.VMEM((levels, width, width), f32),
             pltpu.VMEM((levels, width, width), jnp.bfloat16),
             dma((3,)),

time: 68.9 us -> 63.9 us (0.927)
  Pallas kernels: 65.8 us -> 60.9 us
    pallas_call x1, Pallas kernels: 65.8 us -> 60.9 us  [body(): pl.pallas_call(functools.partial(kernel, (k_count, depth, width, levels,...]
where the time goes in v4:
time: 63.9 us; the launch traced here: 63.5 us
  Pallas kernels  60.9 us (95%)
  local copies, waits for them, and re-layouts  1.95 us (3%)
  between operations  0.64 us (1%)
    pallas_call x1, Pallas kernels, body(): pl.pallas_call(functools.partial(kernel, (k_count, depth, width, levels,...  60.9 us
    unnamed x2, local copies, waits for them, and re-layouts  1.95 us

profile of v4, /device:TPU:8, one launch (start us, length us, event | category | flops | bytes accessed | tf_op | source)
XLA Modules:
  0.0 63.5 jit_solution(12723602909111956848)
XLA Ops:
  0.6 60.9 %shard_map.59 = (f32[32,32,512]{2,1,0:T(8,128)S(1)}, f32[32,512]{1,0:T(8,128)S(1)}) custom-call(f32[32,32,512]{2,1,0:T(8,128)} %field.1, f32[32,32,512]{2,1,0:T(8,128)} %right_side.1, f32[32,512]{1,0:T(8,128)} %kappa.1, bf16[8,512,512]{2,1,0:T(8,128)(2,1)} %fronts.1), custom_call_target="tpu_custom_call" | custom-call | tf_op jit(solution)/shard_map/pallas_call | solution.py:602
  61.5 1.3 %copy.8 = f32[32,32,512]{2,1,0:T(8,128)} copy(f32[32,32,512]{2,1,0:T(8,128)S(1)} %get-tuple-element.4) | data formatting | bytes 4194304
  62.9 0.6 copy.9

commit v5 on v4

--- a/solution.py
+++ b/solution.py
@@ -49,7 +49,7 @@
 def kernel(
     sizes,
     field, right_side, kappa, fronts,
-    residual, separator,
+    residual, mix_here, mix_there, last_turned, last_extra,
     cells, sources, shift, weights, turned, extra, bulk_out, bulk_in,
     first_row, last_row, below, above, edge_left, edge_right,
     rim_first, rim_last, rim_left, rim_right,
@@ -169,17 +169,27 @@
 
     def bulk_start(pair, piece):
         part = pl.ds(piece * PIECE, PIECE)
-        bulk_out[pair, part] = turned[pairs[pair][0], part].astype(jnp.float32)
+        level = pairs[pair][0]
+        block = last_turned[level, part] if level < 2 else turned[level, part]
+        bulk_out[pair, part] = block.astype(jnp.float32)
         bulk(pair, piece).start()
 
     def bulk_take(pair, piece):
         part = pl.ds(piece * PIECE, PIECE)
         bulk(pair, piece).wait_recv()
-        extra[pair, part] = bulk_in[pair, part].astype(jnp.bfloat16)
+        block = bulk_in[pair, part].astype(jnp.bfloat16)
+        if pairs[pair][0] < 2:
+            last_extra[part, :] = block
+        else:
+            extra[pair, part] = block
 
     def turn(level, block):
         part = pl.ds(block * LANES, LANES)
-        turned[level, part, :] = weights[level, :, part].T
+        block = weights[level, :, part].T
+        if level < 2:
+            last_turned[level, part, :] = block
+        else:
+            turned[level, part, :] = block
 
     loads[0].wait()
     first_row[...] = cells[:, 0, :]
@@ -561,14 +571,15 @@
                 else:
                     here = mine - sign(a) * values[0]
                     there = values[1] - sign(a) * values[2]
+                if phase + 1 == phases:
+                    mix_here[part, :] = here.astype(jnp.bfloat16)
+                    mix_there[part, :] = there.astype(jnp.bfloat16)
+                    continue
                 here = times(here, turned[a])
                 there = times(there, extra[spare])
                 product = times(here - sign(b) * there, turned[b])
-            if phase + 1 < phases:
-                send(phase + 1, chunk, product)
-                fill_back(phase + 1, chunk)
-            else:
-                separator[part, :] = product
+            send(phase + 1, chunk, product)
+            fill_back(phase + 1, chunk)
 
     for copy in edge_halos + rim_halos + [above_halo] + below_halos:
         copy.wait_send()
@@ -579,6 +590,25 @@
         for slot in range(len(targets[phase])):
             for chunk in range(CHUNKS):
                 exchange(phase, slot, chunk).wait_send()
+
+
+def finish(here, there, turned, extra, inner, residual, separator, held, copy_sem):
+    copies = [pltpu.make_async_copy(inner, residual, copy_sem.at[0])]
+    copies[0].start()
+
+    def times(state, front):
+        return lax.dot_general(
+            state, front, (((1,), (0,)), ((), ())), preferred_element_type=jnp.float32
+        )
+
+    upper = jnp.bitwise_and(lax.axis_index("col"), 1)
+    sign = 1.0 - 2.0 * upper.astype(jnp.float32)
+    mix = times(here[...], turned[1]) - sign * times(there[...], extra[...])
+    held[...] = times(mix.astype(jnp.bfloat16), turned[0])
+    copies.append(pltpu.make_async_copy(held, separator, copy_sem.at[1]))
+    copies[1].start()
+    for copy in copies:
+        copy.wait()
 
 
 def body(field, right_side, kappa, fronts):
@@ -599,14 +629,17 @@
     edge = pltpu.VMEM((k_count, LANES), f32)
     rim = pltpu.VMEM((depth, LANES), f32)
     arrays = (field, right_side, kappa, fronts)
-    return pl.pallas_call(
+    residual, *rest = pl.pallas_call(
         functools.partial(kernel, (k_count, depth, width, levels, col_bits, n_row, n_col)),
         out_shape=(
             jax.ShapeDtypeStruct((k_count, depth, width), f32),
-            jax.ShapeDtypeStruct((k_count, width), f32),
+            jax.ShapeDtypeStruct((k_count, width), jnp.bfloat16),
+            jax.ShapeDtypeStruct((k_count, width), jnp.bfloat16),
+            jax.ShapeDtypeStruct((2, width, width), jnp.bfloat16),
+            jax.ShapeDtypeStruct((width, width), jnp.bfloat16),
         ),
         in_specs=[pl.BlockSpec(memory_space=pl.ANY)] * 4,
-        out_specs=(pl.BlockSpec(memory_space=pltpu.VMEM),) * 2,
+        out_specs=(pl.BlockSpec(memory_space=pltpu.VMEM),) * 5,
         scratch_shapes=[
             cube,
             cube,
@@ -650,6 +683,17 @@
             collective_id=0, has_side_effects=True, vmem_limit_bytes=48 << 20
         ),
     )(*(pltpu.with_memory_space_constraint(array, pltpu.HBM) for array in arrays))
+    return pl.pallas_call(
+        finish,
+        out_shape=(
+            jax.ShapeDtypeStruct((k_count, depth, width), f32),
+            jax.ShapeDtypeStruct((k_count, width), f32),
+        ),
+        in_specs=[pl.BlockSpec(memory_space=pltpu.VMEM)] * 5,
+        out_specs=(pl.BlockSpec(memory_space=pl.ANY),) * 2,
+        scratch_shapes=[line, dma((2,))],
+        compiler_params=pltpu.CompilerParams(vmem_limit_bytes=8 << 20),
+    )(*rest, residual)
 
 
 def solution(mesh):

time: 63.9 us -> 63 us (0.986)
  local copies, waits for them, and re-layouts: 1.95 us -> 0 us
  Pallas kernels: 60.9 us -> 62 us
    unnamed x2 -> x0, local copies, waits for them, and re-layouts: 1.95 us -> none
    pallas_call x0 -> x1, Pallas kernels: none -> 1.47 us  [body(): pl.pallas_call(finish, out_shape=(jax.ShapeDtypeStruct((k_count, depth, w...]
where the time goes in v5:
time: 63 us; the launch traced here: 62.6 us
  Pallas kernels  62 us (98%)
  between operations  0.64 us (1%)
    pallas_call x1, Pallas kernels, body(): pl.pallas_call(functools.partial(kernel, (k_count, depth, width, levels,...  60.5 us
    pallas_call x1, Pallas kernels, body(): pl.pallas_call(finish, out_shape=(jax.ShapeDtypeStruct((k_count, depth, w...  1.47 us

profile of v5, /device:TPU:8, one launch (start us, length us, event | category | flops | bytes accessed | tf_op | source)
XLA Modules:
  0.0 62.6 jit_solution(3186959431313308726)
XLA Ops:
  0.6 60.5 %shard_map.59 = (f32[32,32,512]{2,1,0:T(8,128)S(1)}, bf16[32,512]{1,0:T(8,128)(2,1)S(1)}, bf16[32,512]{1,0:T(8,128)(2,1)S(1)}, bf16[2,512,512]{2,1,0:T(8,128)(2,1)S(1)}, bf16[512,512]{1,0:T(8,128)(2,1)S(1)}) custom-call(f32[32,32,512]{2,1,0:T(8,128)} %field.1, f32[32,32,512]{2,1,0:T(8,128)} %right_side.1, f32[32,512]{1,0:T(8,128)} %kappa.1, ...), custom_call_target="tpu_custom_call" | custom-call | tf_op jit(solution)/shard_map/pallas_call | solution.py:632
  61.1 1.5 %shard_map.60 = (f32[32,32,512]{2,1,0:T(8,128)}, f32[32,512]{1,0:T(8,128)}) custom-call(bf16[32,512]{1,0:T(8,128)(2,1)S(1)} %get-tuple-element.7.here, bf16[32,512]{1,0:T(8,128)(2,1)S(1)} %get-tuple-element.8.there, bf16[2,512,512]{2,1,0:T(8,128)(2,1)S(1)} %get-tuple-element.9.turned, bf16[512,512]{1,0:T(8,128)(2,1)S(1)} %get-tuple-element.10.extra, ...), custom_call_target="tpu_custom_call" | custom-call | tf_op jit(solution)/shard_map/pallas_call | solution.py:686

commit v6 on v5

--- a/solution.py
+++ b/solution.py
@@ -121,13 +121,6 @@
         for level in range(levels)
     ]
     loads[0].start()
-    front_loads[0].start()
-    loads[1].start()
-    loads[2].start()
-    order = [1, 2] + [a for a, b in pairs if a != 1]
-    order += [level for level in range(1, levels) if level not in order]
-    for level in order:
-        front_loads[level].start()
 
     def halo(slot, source, target, device):
         return pltpu.make_async_remote_copy(
@@ -192,6 +185,13 @@
             turned[level, part, :] = block
 
     loads[0].wait()
+    front_loads[0].start()
+    loads[1].start()
+    loads[2].start()
+    order = [1, 2] + [a for a, b in pairs if a != 1]
+    order += [level for level in range(1, levels) if level not in order]
+    for level in order:
+        front_loads[level].start()
     first_row[...] = cells[:, 0, :]
     last_row[...] = cells[:, depth - 1, :]
     pl.semaphore_wait(barrier, len(friends))
@@ -593,8 +593,14 @@
 
 
 def finish(here, there, turned, extra, inner, residual, separator, held, copy_sem):
-    copies = [pltpu.make_async_copy(inner, residual, copy_sem.at[0])]
-    copies[0].start()
+    quarter = inner.shape[0] // 4
+    copies = []
+    for slot in range(4):
+        part = pl.ds(slot * quarter, quarter)
+        copies.append(
+            pltpu.make_async_copy(inner.at[part], residual.at[part], copy_sem.at[slot])
+        )
+        copies[slot].start()
 
     def times(state, front):
         return lax.dot_general(
@@ -605,8 +611,8 @@
     sign = 1.0 - 2.0 * upper.astype(jnp.float32)
     mix = times(here[...], turned[1]) - sign * times(there[...], extra[...])
     held[...] = times(mix.astype(jnp.bfloat16), turned[0])
-    copies.append(pltpu.make_async_copy(held, separator, copy_sem.at[1]))
-    copies[1].start()
+    copies.append(pltpu.make_async_copy(held, separator, copy_sem.at[4]))
+    copies[4].start()
     for copy in copies:
         copy.wait()
 
@@ -691,7 +697,7 @@
         ),
         in_specs=[pl.BlockSpec(memory_space=pltpu.VMEM)] * 5,
         out_specs=(pl.BlockSpec(memory_space=pl.ANY),) * 2,
-        scratch_shapes=[line, dma((2,))],
+        scratch_shapes=[line, dma((5,))],
         compiler_params=pltpu.CompilerParams(vmem_limit_bytes=8 << 20),
     )(*rest, residual)
 

time: 63 us -> 63.1 us (level)
  no operation moved by 1% of the time
where the time goes in v6:
time: 63.1 us; the launch traced here: 63 us
  Pallas kernels  62.4 us (99%)
  between operations  0.64 us (1%)
    pallas_call x1, Pallas kernels, body(): pl.pallas_call(functools.partial(kernel, (k_count, depth, width, levels,...  60.9 us
    pallas_call x1, Pallas kernels, body(): pl.pallas_call(finish, out_shape=(jax.ShapeDtypeStruct((k_count, depth, w...  1.5 us

profile of v6, /device:TPU:8, one launch (start us, length us, event | category | flops | bytes accessed | tf_op | source)
XLA Modules:
  0.0 63.0 jit_solution(737900315491160377)
XLA Ops:
  0.6 60.9 %shard_map.59 = (f32[32,32,512]{2,1,0:T(8,128)S(1)}, bf16[32,512]{1,0:T(8,128)(2,1)S(1)}, bf16[32,512]{1,0:T(8,128)(2,1)S(1)}, bf16[2,512,512]{2,1,0:T(8,128)(2,1)S(1)}, bf16[512,512]{1,0:T(8,128)(2,1)S(1)}) custom-call(f32[32,32,512]{2,1,0:T(8,128)} %field.1, f32[32,32,512]{2,1,0:T(8,128)} %right_side.1, f32[32,512]{1,0:T(8,128)} %kappa.1, ...), custom_call_target="tpu_custom_call" | custom-call | tf_op jit(solution)/shard_map/pallas_call | solution.py:638
  61.5 1.5 %shard_map.60 = (f32[32,32,512]{2,1,0:T(8,128)}, f32[32,512]{1,0:T(8,128)}) custom-call(bf16[32,512]{1,0:T(8,128)(2,1)S(1)} %get-tuple-element.7.here, bf16[32,512]{1,0:T(8,128)(2,1)S(1)} %get-tuple-element.8.there, bf16[2,512,512]{2,1,0:T(8,128)(2,1)S(1)} %get-tuple-element.9.turned, bf16[512,512]{1,0:T(8,128)(2,1)S(1)} %get-tuple-element.10.extra, ...), custom_call_target="tpu_custom_call" | custom-call | tf_op jit(solution)/shard_map/pallas_call | solution.py:692
